TPU v7x, 512 devices: a whole 4x4x16 slice. The times are simulated.
512 devices in a mesh: lev: 4 (over x_lo, core), tile: 128 (over y, x_hi, z).
Axes of the slice: x: 4 (x_hi: 2, x_lo: 2; x = x_hi * 2 + x_lo), y: 4, z: 16, core: 2. Of those that a mesh axis runs over, the one named last changes fastest.
Arguments:
- forcing: bfloat16 [4, 128, 36, 36, 128], P('lev', 'tile'), may hold values from -6 to 6
- transport: float32 [4, 4, 128, 36, 36], P(None, 'lev', 'tile'), may hold values from 0.04 to 0.22
- reactivity: float32 [4, 128, 36, 36], P('lev', 'tile'), may hold values from 0.1 to 0.6
- jacobian: float32 [4, 128, 128], P('lev'), may hold values from -0.5 to 0.5
- pattern: int32 [8, 8], replicated, may hold values 0 or 1
- lon_rate: float32 [128, 576], P('tile'), may hold values from 0.003 to 0.03
- lat_rate: float32 [128, 288], P('tile'), may hold values from 0.003 to 0.03
- vertical: float32 [128, 4, 4], replicated, may hold values from -3 to 3
- step_scale: float32 [128], replicated, may hold values from 0.3 to 1
- control: bfloat16 [4, 128, 36, 36, 128], P('lev', 'tile'), may hold values from -6 to 6
Outputs:
- control_new: bfloat16 [4, 128, 36, 36, 128], P('lev', 'tile')
All inputs are finite; a program needn't handle non-finite values.
Results may differ from a plain program's by a relative error of at most 0.001.
The roundings to bfloat16 on the way count: a program that leaves them out, or rounds other values in their place, can miss the bound.
Values may be sent and summed in bfloat16 or wider, within the bound.
No kernel may reach another device: no remote copies, remote signals or barrier semaphores. Data moves between devices by JAX's collectives and lax.ppermute only.
A program may use at most 64 MiB of HBM per device.

v0:
```python
import jax
import jax.numpy as jnp
from jax import lax
from jax.experimental import pallas as pl
from jax.experimental.pallas import tpu as pltpu
from jax.sharding import PartitionSpec as P

TJ = 8
TI = 16
STEPS = 3
NX = 36
NY = 36
S = 128
YP = 48
Y0 = 8
YO = 40
FLD = 5
HIGHEST = lax.Precision.HIGHEST
VMEM = pl.BlockSpec(memory_space=pltpu.VMEM)
LON_MASKS = (8, 16, 32, 64)
LAT_MASKS = (1, 2, 4)


def round_factors(me, sums, bits):
    tiles, rows = sums.shape[0], 6 * bits
    row = lax.broadcasted_iota(jnp.int32, (rows, tiles), 0)
    tile = lax.broadcasted_iota(jnp.int32, (rows, tiles), 1)
    level = jnp.zeros_like(row)
    for k in range(1, bits):
        level = level + (row >= 6 * k).astype(jnp.int32)
    kind = row - 6 * level
    here = jnp.full_like(row, me)
    block = lax.shift_right_logical(here, level)
    of_tile = lax.shift_right_logical(tile, level)
    upper = (block & 1) == 1
    own = of_tile == block
    other = of_tile == block + 1 - 2 * (block & 1)
    used = (
        ((kind == 0) & ~upper & other)
        | ((kind == 1) & upper & other)
        | ((kind == 2) & upper & own)
        | ((kind == 3) & ~upper & own)
        | ((kind == 4) & own & (tile < here))
        | ((kind == 5) & own & (tile > here))
    )
    total = jnp.dot(used.astype(jnp.float32), sums, precision=HIGHEST, preferred_element_type=jnp.float32)
    off = ((kind == 4) & ~upper) | ((kind == 5) & upper)
    gate = 1.0 - off.astype(jnp.float32)[:, :1]
    return gate * jnp.exp(-total)


def put_line(state, at, value):
    state[at : at + Y0, :] = jnp.zeros((Y0, S), jnp.float32)
    state[at + YP - 8 : at + YP, :] = jnp.zeros((8, S), jnp.float32)
    first = Y0 - (value.shape[0] - NY) // 2
    state[at + first : at + first + value.shape[0], :] = value


def put_rims(state, south_ref, north_ref, base, lines, skip):
    for j in range(3):
        for ref, row in ((south_ref, Y0 - 3 + j), (north_ref, Y0 + NY + j)):
            rim = ref[j][skip : skip + lines].astype(jnp.float32)
            state[pl.ds(base + row, lines, stride=YP), :] = rim


def put_weights(weights, planes_ref, first, lines):
    for f in range(FLD):
        column = planes_ref[f].T
        for x in range(lines):
            spread = jnp.broadcast_to(column[:YP, first + x : first + x + 1], (YP, S))
            weights[f, x * YP : (x + 1) * YP, :] = spread


def advance(source, weights, large, small, at, wat, lines):
    size = lines * YP
    here = source[at : at + size, :]
    west = source[at - YP : at - YP + size, :]
    east = source[at + YP : at + YP + size, :]
    south = pltpu.roll(here, 1, 0)
    north = pltpu.roll(here, size - 1, 0)
    moved = (
        here
        + weights[0, wat : wat + size, :] * (west - here)
        + weights[1, wat : wat + size, :] * (east - here)
        + weights[2, wat : wat + size, :] * (south - here)
        + weights[3, wat : wat + size, :] * (north - here)
    )
    m1, m2, m3 = split(moved)
    top = jnp.dot(jnp.concatenate([m1, m2], 1), large, preferred_element_type=jnp.float32)
    low = jnp.dot(jnp.concatenate([m3, m1], 1), small, preferred_element_type=jnp.float32)
    reacted = top[:, :S] + (top[:, S:] + low)
    return moved + weights[4, wat : wat + size, :] * reacted


def round_gradient(result, line):
    part = result[line * YP + Y0 : line * YP + Y0 + YO]
    return part.astype(jnp.bfloat16).astype(jnp.float32)


def inner_kernel(
    forcing_ref, south_ref, north_ref, planes_ref, pattern_ref, jacobian_ref,
    gradient_ref, between_ref, large_ref, small_ref,
    even, odd, weights, pattern_copy, jacobian_copy, arrived,
):
    fetches = [
        pltpu.make_async_copy(pattern_ref, pattern_copy, arrived.at[0]),
        pltpu.make_async_copy(jacobian_ref, jacobian_copy, arrived.at[1]),
    ]
    for fetch in fetches:
        fetch.start()
    for x in range(NX):
        put_line(even, x * YP, forcing_ref[x].astype(jnp.float32))
    put_rims(even, south_ref, north_ref, 0, NX, 0)
    put_weights(weights, planes_ref, 0, NX)

    for fetch in fetches:
        fetch.wait()
    blocks = pattern_copy.shape[0]
    spread = (
        lax.broadcasted_iota(jnp.int32, (blocks, S), 0)
        == lax.broadcasted_iota(jnp.int32, (blocks, S), 1) // (S // blocks)
    ).astype(jnp.float32)
    wide = jnp.dot(pattern_copy[...].astype(jnp.float32), spread, preferred_element_type=jnp.float32)
    mask = lax.dot_general(spread, wide, (((0,), (0,)), ((), ())), preferred_element_type=jnp.float32)
    w1, w2, w3 = split(jacobian_copy[...] * mask)
    both = jnp.concatenate([w1, w2], 1)
    large = jnp.concatenate([both, both], 0)
    small = jnp.concatenate([w1, w3], 0)
    large_ref[...] = large
    small_ref[...] = small

    source, target = even, odd
    for step in range(STEPS):
        first, last = 1 + step, NX - 1 - step
        groups = [(x, min(4, last - x)) for x in range(first, last, 4)]
        for x, lines in groups:
            result = advance(source, weights, large, small, x * YP, x * YP, lines)
            if step == STEPS - 1:
                for i in range(lines):
                    gradient_ref[x - 3 + i] = round_gradient(result, i)
            else:
                target[x * YP : (x + lines) * YP, :] = result
        if step < STEPS - 1:
            for i, x in enumerate((1 + step, 2 + step, NX - 3 - step, NX - 2 - step)):
                between_ref[4 * step + i] = target[x * YP : (x + 1) * YP, :]
        source, target = target, source


def outer_kernel(
    forcing_ref, south_ref, north_ref, west_ref, east_ref, planes_ref, between_ref, large_ref, small_ref,
    gradient_ref, zero, one, two, weights,
):
    large, small = large_ref[...], small_ref[...]
    slots = 6
    for side in range(2):
        base = side * slots * YP
        halo = (west_ref, east_ref)[side]
        for i in range(3):
            slot = i if side == 0 else i + 2
            put_line(zero, base + slot * YP, halo[i].astype(jnp.float32))
        first = 0 if side == 0 else NX - 2
        slot = 3 if side == 0 else 0
        for i in range(2):
            put_line(zero, base + (slot + i) * YP, forcing_ref[first + i].astype(jnp.float32))
        put_rims(zero, south_ref, north_ref, base + slot * YP, 2, first)
        put_weights(weights.at[side], planes_ref, 1 if side == 0 else NX, 5)

    def at(side, slot):
        return (side * slots + slot) * YP

    for side in range(2):
        done = advance(zero, weights.at[side], large, small, at(side, 1), 0 if side == 0 else 2 * YP, 3)
        for i in range(3):
            slot = i if side == 0 else i + 2
            one[at(side, slot) : at(side, slot + 1), :] = done[i * YP : (i + 1) * YP]
        for i in range(2):
            slot = i + 3 if side == 0 else i
            one[at(side, slot) : at(side, slot + 1), :] = between_ref[2 * side + i]
    for side in range(2):
        done = advance(one, weights.at[side], large, small, at(side, 1), YP, 3)
        for i in range(3):
            slot = i if side == 0 else i + 2
            two[at(side, slot) : at(side, slot + 1), :] = done[i * YP : (i + 1) * YP]
        for i in range(2):
            slot = i + 3 if side == 0 else i
            two[at(side, slot) : at(side, slot + 1), :] = between_ref[4 + 2 * side + i]
    for side in range(2):
        done = advance(two, weights.at[side], large, small, at(side, 1), 2 * YP if side == 0 else 0, 3)
        for i in range(3):
            gradient_ref[3 * side + i] = round_gradient(done, i)


def split(x):
    high = x.astype(jnp.bfloat16)
    rest = x - high.astype(jnp.float32)
    middle = rest.astype(jnp.bfloat16)
    return high, middle, (rest - middle.astype(jnp.float32)).astype(jnp.bfloat16)


def lon_kernel(
    me_ref, inner_ref, outer_ref, rate_ref, local_ref, edge_ref, lon_ref, lat_ref, lonc_ref, latc_ref
):
    fields = rate_ref[...].T
    row = lax.broadcasted_iota(jnp.int32, (YO, YO), 0)
    col = lax.broadcasted_iota(jnp.int32, (YO, YO), 1)
    upto = (col <= row).astype(jnp.float32)
    after = (col > row).astype(jnp.float32)
    for first, out in ((0, lon_ref), (YO, lat_ref)):
        rates = fields[first : first + YO]
        quarter = jnp.sqrt(jnp.sqrt(rates))
        before = jnp.dot(upto, rates, precision=HIGHEST, preferred_element_type=jnp.float32)
        beyond = jnp.dot(after, rates, precision=HIGHEST, preferred_element_type=jnp.float32)
        out[0] = jnp.exp(-rates)
        out[1] = quarter
        out[2] = quarter * jnp.exp(-before)
        out[3] = quarter * jnp.exp(-beyond)
    lonc_ref[...] = round_factors(me_ref[0] // TJ, fields[2 * YO : 2 * YO + TI], len(LON_MASKS))
    latc_ref[...] = round_factors(me_ref[0] % TJ, fields[2 * YO + TI : 2 * YO + TI + TJ], len(LAT_MASKS))

    def gradient(x):
        if x < 3:
            return outer_ref[x]
        return inner_ref[x - 3] if x < NX - 3 else outer_ref[x - NX + 6]

    held = jnp.zeros((YO, S), jnp.float32)
    for x in range(NX):
        held = lon_ref[0, x : x + 1, :] * held + lon_ref[1, x : x + 1, :] * gradient(x)
        local_ref[x] = held
    edge_ref[0] = held
    held = jnp.zeros((YO, S), jnp.float32)
    for x in range(NX - 1, -1, -1):
        quarter = lon_ref[1, x : x + 1, :]
        local_ref[x] = quarter * (local_ref[x] + held)
        held = lon_ref[0, x : x + 1, :] * (quarter * gradient(x) + held)
    edge_ref[1] = held


def carries(received, coef_ref):
    ahead = jnp.zeros(received[0].shape[1:], jnp.float32)
    behind = ahead
    for k, ref in enumerate(received):
        ahead = ahead + coef_ref[6 * k + 4 : 6 * k + 5, :] * ref[0]
        behind = behind + coef_ref[6 * k + 5 : 6 * k + 6, :] * ref[1]
    return ahead, behind


def lat_kernel(local_ref, r0, r1, r2, r3, coef_ref, lon_ref, lat_ref, out_ref, edge_ref, plane, held_ref):
    ahead_in, behind_in = carries((r0, r1, r2, r3), coef_ref)

    def along_lon(x, carry):
        at = pl.multiple_of(x * YO, 8)
        plane[pl.ds(at, YO), :] = (
            local_ref[x]
            + lon_ref[2, pl.ds(x, 1), :] * ahead_in
            + lon_ref[3, pl.ds(x, 1), :] * behind_in
        )
        return carry

    lax.fori_loop(0, NX, along_lon, 0, unroll=2)
    held = jnp.zeros((NX, S), jnp.float32)
    for y in range(NY):
        held = lat_ref[0, y : y + 1, :] * held + lat_ref[1, y : y + 1, :] * plane[pl.ds(y, NX, stride=YO), :]
        held_ref[y] = held
    edge_ref[0, :NX, :] = held
    edge_ref[0, NX:, :] = jnp.zeros((YO - NX, S), jnp.float32)
    held = jnp.zeros((NX, S), jnp.float32)
    for y in range(NY - 1, -1, -1):
        quarter = lat_ref[1, y : y + 1, :]
        value = plane[pl.ds(y, NX, stride=YO), :]
        out_ref[pl.ds(y, NX, stride=YO), :] = quarter * (held_ref[y] + held)
        held = lat_ref[0, y : y + 1, :] * (quarter * value + held)
    edge_ref[1, :NX, :] = held
    edge_ref[1, NX:, :] = jnp.zeros((YO - NX, S), jnp.float32)


def finish_kernel(local_ref, r0, r1, r2, coef_ref, lat_ref, out_ref, carry_ref):
    carry_ref[0], carry_ref[1] = carries((r0, r1, r2), coef_ref)
    ahead, behind = lat_ref[2][:NY], lat_ref[3][:NY]

    def line(x, carry):
        at = pl.multiple_of(x * YO, 8)
        value = (
            local_ref[pl.ds(at, NY), :]
            + ahead * carry_ref[0, pl.ds(x, 1), :]
            + behind * carry_ref[1, pl.ds(x, 1), :]
        )
        out_ref[x] = value.astype(jnp.bfloat16)
        return carry

    lax.fori_loop(0, NX, line, 0, unroll=2)


def call(kernel, outs, scratch=(), specs=None):
    def run(*operands):
        return built(len(operands))(*operands)

    def built(count):
        return pl.pallas_call(
        kernel,
        out_shape=outs,
        in_specs=specs or [VMEM] * count,
        scratch_shapes=list(scratch),
        compiler_params=pltpu.CompilerParams(vmem_limit_bytes=40 * 2**20),
    )

    return run


def f32(*shape):
    return jax.ShapeDtypeStruct(shape, jnp.float32)


def swap(x, axis, mask):
    return lax.ppermute(x, axis, [(i, i ^ mask) for i in range(lax.axis_size(axis))])


def three_parts(x):
    high = lax.reduce_precision(x, 8, 7)
    rest = x - high
    middle = lax.reduce_precision(rest, 8, 7)
    low = rest - middle
    return jnp.concatenate([high, middle, low], 0).astype(jnp.bfloat16)


def join_parts(parts):
    third = parts.shape[0] // 3
    parts = parts.astype(jnp.float32)
    return (parts[:third] + parts[third : 2 * third]) + parts[2 * third :]


def widen(coefs, before, after):
    return jnp.pad(coefs, ((0, 0), (before, after), (Y0 - 2, S - NY - 2 - Y0)))


def pack(cells, coefs):
    wide = jnp.pad(coefs, ((0, 0), (0, S - coefs.shape[1])))
    return jnp.concatenate([cells.reshape(-1, S), three_parts(wide)], 0)


def unpack(rows, n, m, w):
    return rows[: n * m].reshape(n, m, S), join_parts(rows[n * m :])[:, :w]


def rate_rows(lon_rate, lat_rate):
    lon = lon_rate[0].reshape(TI, 1, NX)
    lat = lat_rate[0].reshape(1, TJ, NY)
    shape = (TI, TJ)
    columns = [
        jnp.broadcast_to(lon, shape + (NX,)),
        jnp.zeros(shape + (YO - NX,), jnp.float32),
        jnp.broadcast_to(lat, shape + (NY,)),
        jnp.zeros(shape + (YO - NY,), jnp.float32),
        jnp.broadcast_to(jnp.sum(lon, 2).reshape(1, 1, TI), shape + (TI,)),
        jnp.broadcast_to(jnp.sum(lat, 2).reshape(1, 1, TJ), shape + (TJ,)),
        jnp.zeros(shape + (S - 2 * YO - TI - TJ,), jnp.float32),
    ]
    return jnp.concatenate(columns, 2).reshape(TI * TJ, S)


def one_device(
    forcing, transport, reactivity, jacobian, pattern, lon_rate, lat_rate, vertical, step_scale, control
):
    cells = forcing[0, 0]
    tile = lax.axis_index("tile")
    tiles = TI * TJ

    coefs = jnp.concatenate([transport[:, 0, 0], reactivity[0, 0][None]], 0)
    northward = pack(
        jnp.swapaxes(cells[:, NY - 3 :], 0, 1),
        jnp.swapaxes(coefs[:, :, NY - 2 :], 1, 2).reshape(2 * FLD, NX),
    )
    southward = pack(
        jnp.swapaxes(cells[:, :3], 0, 1), jnp.swapaxes(coefs[:, :, :2], 1, 2).reshape(2 * FLD, NX)
    )
    steps_up = [(i, i + 1) for i in range(tiles) if i % TJ < TJ - 1]
    from_south = lax.ppermute(northward, "tile", steps_up)
    from_north = lax.ppermute(southward, "tile", [(b, a) for a, b in steps_up])
    south, south_coefs = unpack(from_south, 3, NX, NX)
    north, north_coefs = unpack(from_north, 3, NX, NX)
    south_coefs, north_coefs, sent = lax.optimization_barrier(
        (south_coefs, north_coefs, rate_rows(lon_rate, lat_rate))
    )
    rates = lax.all_to_all(sent, "tile", split_axis=0, concat_axis=0, tiled=True)
    south_coefs = jnp.swapaxes(south_coefs.reshape(FLD, 2, NX), 1, 2)
    north_coefs = jnp.swapaxes(north_coefs.reshape(FLD, 2, NX), 1, 2)
    tall = jnp.concatenate([south_coefs, coefs, north_coefs], 2)

    def side(lines):
        return jnp.concatenate(
            [jnp.swapaxes(south[1:, lines], 0, 1), cells[lines], jnp.swapaxes(north[:2, lines], 0, 1)], 1
        )

    eastward = pack(side(slice(NX - 3, NX)), tall[:, NX - 2 :].reshape(2 * FLD, NY + 4))
    westward = pack(side(slice(0, 3)), tall[:, :2].reshape(2 * FLD, NY + 4))
    from_west = lax.ppermute(eastward, "tile", [(i, (i + TJ) % tiles) for i in range(tiles)])
    from_east = lax.ppermute(westward, "tile", [((i + TJ) % tiles, i) for i in range(tiles)])
    inner, between, large, small = call(
        inner_kernel,
        (
            f32(NX - 6, YO, S),
            f32(8, YP, S),
            jax.ShapeDtypeStruct((2 * S, 2 * S), jnp.bfloat16),
            jax.ShapeDtypeStruct((2 * S, S), jnp.bfloat16),
        ),
        (
            pltpu.VMEM((NX * YP, S), jnp.float32),
            pltpu.VMEM((NX * YP, S), jnp.float32),
            pltpu.VMEM((FLD, NX * YP, S), jnp.float32),
            pltpu.VMEM(pattern.shape, pattern.dtype),
            pltpu.VMEM((S, S), jnp.float32),
            pltpu.SemaphoreType.DMA((2,)),
        ),
        specs=[VMEM] * 4 + [pl.BlockSpec(memory_space=pl.ANY)] * 2,
    )(cells, south, north, widen(tall, 0, YP - NX), pattern, jacobian[0])
    west, west_coefs = unpack(from_west, 3, NY + 4, NY + 4)
    east, east_coefs = unpack(from_east, 3, NY + 4, NY + 4)
    planes = jnp.concatenate(
        [west_coefs.reshape(FLD, 2, NY + 4), tall, east_coefs.reshape(FLD, 2, NY + 4)], 1
    )
    planes = widen(planes, 1, YP - NX - 5)

    outer = call(
        outer_kernel,
        f32(6, YO, S),
        tuple(pltpu.VMEM((12 * YP, S), jnp.float32) for _ in range(3))
        + (pltpu.VMEM((2, FLD, 5 * YP, S), jnp.float32),),
    )(cells, south, north, west, east, planes, between, large, small)
    local, edge, lon, lat, lon_coef, lat_coef = call(
        lon_kernel,
        (f32(NX, YO, S), f32(2, YO, S), f32(4, YO, S), f32(4, YO, S), f32(6 * 4, S), f32(6 * 3, S)),
        specs=[pl.BlockSpec(memory_space=pltpu.SMEM), VMEM, VMEM, VMEM],
    )(tile.reshape(1), inner, outer, rates)

    def rounds(edge, coef, bits):
        received = []
        for k, mask in enumerate(bits):
            other = swap(edge, "tile", mask)
            received.append(other)
            if k + 1 < len(bits):
                mine = coef[6 * k : 6 * k + 2][:, None]
                theirs = coef[6 * k + 2 : 6 * k + 4][:, None]
                edge = mine * edge + theirs * other
        return received

    level_here = lax.axis_index("lev")
    mixing = lax.dynamic_index_in_dim(vertical, level_here, 1, keepdims=False).T
    factors = [
        step_scale * lax.dynamic_index_in_dim(mixing, level_here ^ mask, 0, keepdims=False)
        for mask in range(4)
    ]
    received = rounds(edge, lon_coef, LON_MASKS)
    received[0], *factors = lax.optimization_barrier((received[0], *factors))
    local, edge = call(
        lat_kernel,
        (f32(NX * YO, S), f32(2, YO, S)),
        (pltpu.VMEM((NX * YO, S), jnp.float32), pltpu.VMEM((NY, NX, S), jnp.float32)),
    )(local, *received, lon_coef, lon, lat)
    filtered = call(
        finish_kernel,
        jax.ShapeDtypeStruct((NX, NY, S), jnp.bfloat16),
        (pltpu.VMEM((2, YO, S), jnp.float32),),
    )(local, *rounds(edge, lat_coef, LAT_MASKS), lat_coef, lat)

    levels = [filtered, swap(filtered, "lev", 1), swap(filtered, "lev", 2)]
    levels.append(swap(levels[2], "lev", 1))
    increment = jnp.zeros((NX, NY, S), jnp.float32)
    for factor, plane in zip(factors, levels):
        increment = increment + factor * plane.astype(jnp.float32)
    updated = control[0, 0].astype(jnp.float32) - increment
    return updated.astype(jnp.bfloat16)[None, None]


def solution(mesh):
    in_specs = (
        P("lev", "tile", None, None, None),
        P(None, "lev", "tile", None, None),
        P("lev", "tile", None, None),
        P("lev", None, None),
        P(),
        P("tile", None),
        P("tile", None),
        P(),
        P(),
        P("lev", "tile", None, None, None),
    )
    out_specs = P("lev", "tile", None, None, None)
    return jax.shard_map(one_device, mesh=mesh, in_specs=in_specs, out_specs=out_specs, check_vma=False)
```

profile of v0, /device:TPU:1, one launch (start us, length us, event | category | flops | bytes accessed | tf_op | source)
XLA Modules:
  0.0 140.6 jit_solution(46236967044551237)
XLA Ops:
  2.0 1.3 collective-permute-start.1
  3.5 5.0 %collective-permute-start = (bf16[138,128]{1,0:T(8,128)(2,1)S(1)}, bf16[138,128]{1,0:T(8,128)(2,1)S(1)}, u32[]{:S(2)}, u32[]{:S(2)}) collective-permute-start(bf16[138,128]{1,0:T(8,128)(2,1)S(1)} %pad_maximum_fusion.3), channel_id=1, source_target_pairs={{0,1},{1,2},{2,3},{3,4},{4,5},{5,6},{6,7},{8,9},{9,10},{10,11},{11... | collective-permute-start | bytes 105992 | tf_op jit(solution)/shard_map/ppermute | solution.py:376
  11.8 15.3 %collective-permute-start.2 = (bf16[150,128]{1,0:T(8,128)(2,1)S(1)}, bf16[150,128]{1,0:T(8,128)(2,1)S(1)}, u32[]{:S(2)}, u32[]{:S(2)}) collective-permute-start(bf16[150,128]{1,0:T(8,128)(2,1)S(1)} %pad_maximum_fusion.1), channel_id=1, source_target_pairs={{0,8},{1,9},{2,10},{3,11},{4,12},{5,13},{6,14},{7,15},{8,16},{9,17... | collective-permute-start | bytes 115208 | tf_op jit(solution)/shard_map/ppermute | solution.py:395
  27.2 6.8 %collective-permute-start.3 = (bf16[150,128]{1,0:T(8,128)(2,1)S(1)}, bf16[150,128]{1,0:T(8,128)(2,1)S(1)}, u32[]{:S(2)}, u32[]{:S(2)}) collective-permute-start(bf16[150,128]{1,0:T(8,128)(2,1)S(1)} %pad_maximum_fusion.2), channel_id=1, source_target_pairs={{8,0},{9,1},{10,2},{11,3},{12,4},{13,5},{14,6},{15,7},{16,8},{17,9... | collective-permute-start | bytes 115208 | tf_op jit(solution)/shard_map/ppermute | solution.py:396
  34.1 14.0 %all-to-all-start = ((f32[128,1,128]{2,1,0:T(1,128)}), f32[128,1,128]{2,1,0:T(1,128)S(1)}, u32[]{:S(2)}, u32[]{:S(2)}) async-start(f32[128,1,128]{2,1,0:T(1,128)} %bitcast.23), calls=%async_computation | async-start | bytes 131072 | tf_op jit(solution)/shard_map/all_to_all | solution.py:383
  48.1 4.1 %shard_map.100 = (f32[30,40,128]{2,1,0:T(8,128)S(1)}, f32[8,48,128]{2,1,0:T(8,128)S(1)}, bf16[256,256]{1,0:T(8,128)(2,1)S(1)}, bf16[256,128]{1,0:T(8,128)(2,1)S(1)}) custom-call(bf16[36,36,128]{2,1,0:T(8,128)(2,1)S(1)} %bitcast.58, bf16[3,36,128]{2,1,0:T(8,128)(2,1)S(1)} %reshape.105.south_ref, bf16[3,36,128]{2,1,0:T(8,128)(2,1)S(1)} %reshape.108.north_ref, ...), custom_call_target="tpu_custom_call" | custom-call | tf_op jit(solution)/shard_map/pallas_call | solution.py:295
  53.5 10.5 %all-to-all-done = f32[128,1,128]{2,1,0:T(1,128)S(1)} async-done(((f32[128,1,128]{2,1,0:T(1,128)}), f32[128,1,128]{2,1,0:T(1,128)S(1)}, u32[]{:S(2)}, u32[]{:S(2)}) %all-to-all-start) | async-done | bytes 65568 | tf_op jit(solution)/shard_map/all_to_all | solution.py:383
  64.4 2.3 %collective-permute-start.4 = (f32[2,40,128]{2,1,0:T(8,128)S(1)}, f32[2,40,128]{2,1,0:T(8,128)S(1)}, u32[]{:S(2)}, u32[]{:S(2)}) collective-permute-start(f32[2,40,128]{2,1,0:T(8,128)S(1)} %get-tuple-element.32), channel_id=1, source_target_pairs={{0,8},{1,9},{2,10},{3,11},{4,12},{5,13},{6,14},{7,15},{8,0},{9,1},... | collective-permute-start | bytes 122888 | tf_op jit(solution)/shard_map/ppermute | solution.py:314
  66.8 11.2 %collective-permute-done.4.r0 = f32[2,40,128]{2,1,0:T(8,128)S(1)} collective-permute-done((f32[2,40,128]{2,1,0:T(8,128)S(1)}, f32[2,40,128]{2,1,0:T(8,128)S(1)}, u32[]{:S(2)}, u32[]{:S(2)}) %collective-permute-start.4) | collective-permute-done | bytes 40992 | tf_op jit(solution)/shard_map/ppermute | solution.py:314
  78.0 2.9 %collective-permute-start.5 = (f32[2,40,128]{2,1,0:T(8,128)S(1)}, f32[2,40,128]{2,1,0:T(8,128)S(1)}, u32[]{:S(2)}, u32[]{:S(2)}) collective-permute-start(f32[2,40,128]{2,1,0:T(8,128)S(1)} %multiply_add_fusion.4), channel_id=1, source_target_pairs={{0,16},{1,17},{2,18},{3,19},{4,20},{5,21},{6,22},{7,23},{8,24},{9,... | collective-permute-start | bytes 122888 | tf_op jit(solution)/shard_map/ppermute | solution.py:314
  80.9 3.3 %collective-permute-done.5.r1 = f32[2,40,128]{2,1,0:T(8,128)S(1)} collective-permute-done((f32[2,40,128]{2,1,0:T(8,128)S(1)}, f32[2,40,128]{2,1,0:T(8,128)S(1)}, u32[]{:S(2)}, u32[]{:S(2)}) %collective-permute-start.5) | collective-permute-done | bytes 40992 | tf_op jit(solution)/shard_map/ppermute | solution.py:314
  84.2 2.4 %collective-permute-start.6 = (f32[2,40,128]{2,1,0:T(8,128)S(1)}, f32[2,40,128]{2,1,0:T(8,128)S(1)}, u32[]{:S(2)}, u32[]{:S(2)}) collective-permute-start(f32[2,40,128]{2,1,0:T(8,128)S(1)} %multiply_add_fusion.3), channel_id=1, source_target_pairs={{0,32},{1,33},{2,34},{3,35},{4,36},{5,37},{6,38},{7,39},{8,40},{9,... | collective-permute-start | bytes 122888 | tf_op jit(solution)/shard_map/ppermute | solution.py:314
  86.7 2.6 %collective-permute-done.6.r2 = f32[2,40,128]{2,1,0:T(8,128)S(1)} collective-permute-done((f32[2,40,128]{2,1,0:T(8,128)S(1)}, f32[2,40,128]{2,1,0:T(8,128)S(1)}, u32[]{:S(2)}, u32[]{:S(2)}) %collective-permute-start.6) | collective-permute-done | bytes 40992 | tf_op jit(solution)/shard_map/ppermute | solution.py:314
  89.3 3.0 %collective-permute-start.7 = (f32[2,40,128]{2,1,0:T(8,128)S(1)}, f32[2,40,128]{2,1,0:T(8,128)S(1)}, u32[]{:S(2)}, u32[]{:S(2)}) collective-permute-start(f32[2,40,128]{2,1,0:T(8,128)S(1)} %multiply_add_fusion.2), channel_id=1, source_target_pairs={{0,64},{1,65},{2,66},{3,67},{4,68},{5,69},{6,70},{7,71},{8,72},{9,... | collective-permute-start | bytes 122888 | tf_op jit(solution)/shard_map/ppermute | solution.py:314
  93.1 2.7 %collective-permute-done.7.r3 = f32[2,40,128]{2,1,0:T(8,128)S(1)} collective-permute-done((f32[2,40,128]{2,1,0:T(8,128)S(1)}, f32[2,40,128]{2,1,0:T(8,128)S(1)}, u32[]{:S(2)}, u32[]{:S(2)}) %collective-permute-start.7) | collective-permute-done | bytes 40992 | tf_op jit(solution)/shard_map/ppermute | solution.py:314
  96.3 3.1 %collective-permute-start.8 = (f32[2,40,128]{2,1,0:T(8,128)S(1)}, f32[2,40,128]{2,1,0:T(8,128)S(1)}, u32[]{:S(2)}, u32[]{:S(2)}) collective-permute-start(f32[2,40,128]{2,1,0:T(8,128)S(1)} %get-tuple-element.40), channel_id=1, source_target_pairs={{0,1},{1,0},{2,3},{3,2},{4,5},{5,4},{6,7},{7,6},{8,9},{9,8},{10,11... | collective-permute-start | bytes 122888 | tf_op jit(solution)/shard_map/ppermute | solution.py:314
  99.5 1.6 %collective-permute-done.8.r0 = f32[2,40,128]{2,1,0:T(8,128)S(1)} collective-permute-done((f32[2,40,128]{2,1,0:T(8,128)S(1)}, f32[2,40,128]{2,1,0:T(8,128)S(1)}, u32[]{:S(2)}, u32[]{:S(2)}) %collective-permute-start.8) | collective-permute-done | bytes 40992 | tf_op jit(solution)/shard_map/ppermute | solution.py:314
  101.1 2.4 %collective-permute-start.9 = (f32[2,40,128]{2,1,0:T(8,128)S(1)}, f32[2,40,128]{2,1,0:T(8,128)S(1)}, u32[]{:S(2)}, u32[]{:S(2)}) collective-permute-start(f32[2,40,128]{2,1,0:T(8,128)S(1)} %multiply_add_fusion.1), channel_id=1, source_target_pairs={{0,2},{1,3},{2,0},{3,1},{4,6},{5,7},{6,4},{7,5},{8,10},{9,11},{10,... | collective-permute-start | bytes 122888 | tf_op jit(solution)/shard_map/ppermute | solution.py:314
  103.5 3.2 %collective-permute-done.9.r1 = f32[2,40,128]{2,1,0:T(8,128)S(1)} collective-permute-done((f32[2,40,128]{2,1,0:T(8,128)S(1)}, f32[2,40,128]{2,1,0:T(8,128)S(1)}, u32[]{:S(2)}, u32[]{:S(2)}) %collective-permute-start.9) | collective-permute-done | bytes 40992 | tf_op jit(solution)/shard_map/ppermute | solution.py:314
  106.8 2.4 %collective-permute-start.10 = (f32[2,40,128]{2,1,0:T(8,128)S(1)}, f32[2,40,128]{2,1,0:T(8,128)S(1)}, u32[]{:S(2)}, u32[]{:S(2)}) collective-permute-start(f32[2,40,128]{2,1,0:T(8,128)S(1)} %multiply_add_fusion), channel_id=1, source_target_pairs={{0,4},{1,5},{2,6},{3,7},{4,0},{5,1},{6,2},{7,3},{8,12},{9,13},{10,... | collective-permute-start | bytes 122888 | tf_op jit(solution)/shard_map/ppermute | solution.py:314
  109.1 6.7 %collective-permute-done.10.r2 = f32[2,40,128]{2,1,0:T(8,128)S(1)} collective-permute-done((f32[2,40,128]{2,1,0:T(8,128)S(1)}, f32[2,40,128]{2,1,0:T(8,128)S(1)}, u32[]{:S(2)}, u32[]{:S(2)}) %collective-permute-start.10) | collective-permute-done | bytes 40992 | tf_op jit(solution)/shard_map/ppermute | solution.py:314
  116.1 2.2 %collective-permute-start.12 = (bf16[36,36,128]{2,1,0:T(8,128)(2,1)S(1)}, bf16[36,36,128]{2,1,0:T(8,128)(2,1)S(1)}, u32[]{:S(2)}, u32[]{:S(2)}) collective-permute-start(bf16[36,36,128]{2,1,0:T(8,128)(2,1)S(1)} %shard_map.104), channel_id=1, source_target_pairs={{0,256},{128,384},{256,0},{384,128},{1,257},{129,385},{257,1},{385... | collective-permute-start | bytes 995336 | tf_op jit(solution)/shard_map/ppermute | solution.py:314
  118.3 13.0 %collective-permute-start.11 = (bf16[36,36,128]{2,1,0:T(8,128)(2,1)S(1)}, bf16[36,36,128]{2,1,0:T(8,128)(2,1)S(1)}, u32[]{:S(2)}, u32[]{:S(2)}) collective-permute-start(bf16[36,36,128]{2,1,0:T(8,128)(2,1)S(1)} %shard_map.104), channel_id=1, source_target_pairs={{0,128},{128,0},{256,384},{384,256},{1,129},{129,1},{257,385},{385... | collective-permute-start | bytes 995336 | tf_op jit(solution)/shard_map/ppermute | solution.py:314
  131.3 6.9 %collective-permute-start.13 = (bf16[36,36,128]{2,1,0:T(8,128)(2,1)S(1)}, bf16[36,36,128]{2,1,0:T(8,128)(2,1)S(1)}, u32[]{:S(2)}, u32[]{:S(2)}) collective-permute-start(bf16[36,36,128]{2,1,0:T(8,128)(2,1)S(1)} %collective-permute-done.12), channel_id=1, source_target_pairs={{0,128},{128,0},{256,384},{384,256},{1,129},{129,1},{257,385},{385... | collective-permute-start | bytes 995336 | tf_op jit(solution)/shard_map/ppermute | solution.py:314
  (107 shorter events, 10.9 us)
Async XLA Ops:
  0.0 0.9 copy-start.4
  0.9 1.0 copy-start
  2.0 9.1 %collective-permute-start.1 = (bf16[138,128]{1,0:T(8,128)(2,1)S(1)}, bf16[138,128]{1,0:T(8,128)(2,1)S(1)}, u32[]{:S(2)}, u32[]{:S(2)}) collective-permute-start(bf16[138,128]{1,0:T(8,128)(2,1)S(1)} %pad_maximum_fusion.4), channel_id=1, source_target_pairs={{1,0},{2,1},{3,2},{4,3},{5,4},{6,5},{7,6},{9,8},{10,9},{11,10},{12... | collective-permute-start | bytes 105992 | tf_op jit(solution)/shard_map/ppermute | solution.py:377
  3.5 7.6 %collective-permute-start = (bf16[138,128]{1,0:T(8,128)(2,1)S(1)}, bf16[138,128]{1,0:T(8,128)(2,1)S(1)}, u32[]{:S(2)}, u32[]{:S(2)}) collective-permute-start(bf16[138,128]{1,0:T(8,128)(2,1)S(1)} %pad_maximum_fusion.3), channel_id=1, source_target_pairs={{0,1},{1,2},{2,3},{3,4},{4,5},{5,6},{6,7},{8,9},{9,10},{10,11},{11... | collective-permute-start | bytes 105992 | tf_op jit(solution)/shard_map/ppermute | solution.py:376
  8.5 0.7 copy-start.5
  9.2 0.7 copy-start.6
  11.8 40.4 %collective-permute-start.2 = (bf16[150,128]{1,0:T(8,128)(2,1)S(1)}, bf16[150,128]{1,0:T(8,128)(2,1)S(1)}, u32[]{:S(2)}, u32[]{:S(2)}) collective-permute-start(bf16[150,128]{1,0:T(8,128)(2,1)S(1)} %pad_maximum_fusion.1), channel_id=1, source_target_pairs={{0,8},{1,9},{2,10},{3,11},{4,12},{5,13},{6,14},{7,15},{8,16},{9,17... | collective-permute-start | bytes 115208 | tf_op jit(solution)/shard_map/ppermute | solution.py:395
  27.2 25.0 %collective-permute-start.3 = (bf16[150,128]{1,0:T(8,128)(2,1)S(1)}, bf16[150,128]{1,0:T(8,128)(2,1)S(1)}, u32[]{:S(2)}, u32[]{:S(2)}) collective-permute-start(bf16[150,128]{1,0:T(8,128)(2,1)S(1)} %pad_maximum_fusion.2), channel_id=1, source_target_pairs={{8,0},{9,1},{10,2},{11,3},{12,4},{13,5},{14,6},{15,7},{16,8},{17,9... | collective-permute-start | bytes 115208 | tf_op jit(solution)/shard_map/ppermute | solution.py:396
  34.1 14.0 %copy-start.1 = (f32[1,128,128]{2,1,0:T(8,128)S(1)}, f32[1,128,128]{2,1,0:T(8,128)}, u32[]{:S(2)}) copy-start(f32[1,128,128]{2,1,0:T(8,128)} %param.13) | copy-start | bytes 196612
  34.1 14.0 %copy-start.2 = (s32[8,8]{1,0:T(8,128)S(1)}, s32[8,8]{1,0:T(8,128)}, u32[]{:S(2)}) copy-start(s32[8,8]{1,0:T(8,128)} %pattern_ref.1) | copy-start | bytes 772
  34.1 29.9 %all-to-all-start = ((f32[128,1,128]{2,1,0:T(1,128)}), f32[128,1,128]{2,1,0:T(1,128)S(1)}, u32[]{:S(2)}, u32[]{:S(2)}) async-start(f32[128,1,128]{2,1,0:T(1,128)} %bitcast.23), calls=%async_computation | async-start | bytes 131072 | tf_op jit(solution)/shard_map/all_to_all | solution.py:383
  64.4 13.5 %collective-permute-start.4 = (f32[2,40,128]{2,1,0:T(8,128)S(1)}, f32[2,40,128]{2,1,0:T(8,128)S(1)}, u32[]{:S(2)}, u32[]{:S(2)}) collective-permute-start(f32[2,40,128]{2,1,0:T(8,128)S(1)} %get-tuple-element.32), channel_id=1, source_target_pairs={{0,8},{1,9},{2,10},{3,11},{4,12},{5,13},{6,14},{7,15},{8,0},{9,1},... | collective-permute-start | bytes 122888 | tf_op jit(solution)/shard_map/ppermute | solution.py:314
  78.0 6.3 %collective-permute-start.5 = (f32[2,40,128]{2,1,0:T(8,128)S(1)}, f32[2,40,128]{2,1,0:T(8,128)S(1)}, u32[]{:S(2)}, u32[]{:S(2)}) collective-permute-start(f32[2,40,128]{2,1,0:T(8,128)S(1)} %multiply_add_fusion.4), channel_id=1, source_target_pairs={{0,16},{1,17},{2,18},{3,19},{4,20},{5,21},{6,22},{7,23},{8,24},{9,... | collective-permute-start | bytes 122888 | tf_op jit(solution)/shard_map/ppermute | solution.py:314
  84.2 5.0 %collective-permute-start.6 = (f32[2,40,128]{2,1,0:T(8,128)S(1)}, f32[2,40,128]{2,1,0:T(8,128)S(1)}, u32[]{:S(2)}, u32[]{:S(2)}) collective-permute-start(f32[2,40,128]{2,1,0:T(8,128)S(1)} %multiply_add_fusion.3), channel_id=1, source_target_pairs={{0,32},{1,33},{2,34},{3,35},{4,36},{5,37},{6,38},{7,39},{8,40},{9,... | collective-permute-start | bytes 122888 | tf_op jit(solution)/shard_map/ppermute | solution.py:314
  89.3 3.0 %copy-start.7 = (f32[128]{0:T(128)S(1)}, f32[128]{0:T(128)}, u32[]{:S(2)}) copy-start(f32[128]{0:T(128)} %param.18) | copy-start | bytes 1540
  89.3 6.5 %collective-permute-start.7 = (f32[2,40,128]{2,1,0:T(8,128)S(1)}, f32[2,40,128]{2,1,0:T(8,128)S(1)}, u32[]{:S(2)}, u32[]{:S(2)}) collective-permute-start(f32[2,40,128]{2,1,0:T(8,128)S(1)} %multiply_add_fusion.2), channel_id=1, source_target_pairs={{0,64},{1,65},{2,66},{3,67},{4,68},{5,69},{6,70},{7,71},{8,72},{9,... | collective-permute-start | bytes 122888 | tf_op jit(solution)/shard_map/ppermute | solution.py:314
  96.3 4.7 %collective-permute-start.8 = (f32[2,40,128]{2,1,0:T(8,128)S(1)}, f32[2,40,128]{2,1,0:T(8,128)S(1)}, u32[]{:S(2)}, u32[]{:S(2)}) collective-permute-start(f32[2,40,128]{2,1,0:T(8,128)S(1)} %get-tuple-element.40), channel_id=1, source_target_pairs={{0,1},{1,0},{2,3},{3,2},{4,5},{5,4},{6,7},{7,6},{8,9},{9,8},{10,11... | collective-permute-start | bytes 122888 | tf_op jit(solution)/shard_map/ppermute | solution.py:314
  101.1 5.6 %collective-permute-start.9 = (f32[2,40,128]{2,1,0:T(8,128)S(1)}, f32[2,40,128]{2,1,0:T(8,128)S(1)}, u32[]{:S(2)}, u32[]{:S(2)}) collective-permute-start(f32[2,40,128]{2,1,0:T(8,128)S(1)} %multiply_add_fusion.1), channel_id=1, source_target_pairs={{0,2},{1,3},{2,0},{3,1},{4,6},{5,7},{6,4},{7,5},{8,10},{9,11},{10,... | collective-permute-start | bytes 122888 | tf_op jit(solution)/shard_map/ppermute | solution.py:314
  106.8 9.1 %collective-permute-start.10 = (f32[2,40,128]{2,1,0:T(8,128)S(1)}, f32[2,40,128]{2,1,0:T(8,128)S(1)}, u32[]{:S(2)}, u32[]{:S(2)}) collective-permute-start(f32[2,40,128]{2,1,0:T(8,128)S(1)} %multiply_add_fusion), channel_id=1, source_target_pairs={{0,4},{1,5},{2,6},{3,7},{4,0},{5,1},{6,2},{7,3},{8,12},{9,13},{10,... | collective-permute-start | bytes 122888 | tf_op jit(solution)/shard_map/ppermute | solution.py:314
  115.8 23.7 %copy-start.3 = (bf16[1,1,36,36,128]{4,3,2,1,0:T(8,128)(2,1)S(1)}, bf16[1,1,36,36,128]{4,3,2,1,0:T(8,128)(2,1)}, u32[]{:S(2)}) copy-start(bf16[1,1,36,36,128]{4,3,2,1,0:T(8,128)(2,1)} %param.19) | copy-start | bytes 995332
  116.1 15.3 %collective-permute-start.12 = (bf16[36,36,128]{2,1,0:T(8,128)(2,1)S(1)}, bf16[36,36,128]{2,1,0:T(8,128)(2,1)S(1)}, u32[]{:S(2)}, u32[]{:S(2)}) collective-permute-start(bf16[36,36,128]{2,1,0:T(8,128)(2,1)S(1)} %shard_map.104), channel_id=1, source_target_pairs={{0,256},{128,384},{256,0},{384,128},{1,257},{129,385},{257,1},{385... | collective-permute-start | bytes 995336 | tf_op jit(solution)/shard_map/ppermute | solution.py:314
  118.3 19.9 %collective-permute-start.11 = (bf16[36,36,128]{2,1,0:T(8,128)(2,1)S(1)}, bf16[36,36,128]{2,1,0:T(8,128)(2,1)S(1)}, u32[]{:S(2)}, u32[]{:S(2)}) collective-permute-start(bf16[36,36,128]{2,1,0:T(8,128)(2,1)S(1)} %shard_map.104), channel_id=1, source_target_pairs={{0,128},{128,0},{256,384},{384,256},{1,129},{129,1},{257,385},{385... | collective-permute-start | bytes 995336 | tf_op jit(solution)/shard_map/ppermute | solution.py:314
  131.3 8.2 %collective-permute-start.13 = (bf16[36,36,128]{2,1,0:T(8,128)(2,1)S(1)}, bf16[36,36,128]{2,1,0:T(8,128)(2,1)S(1)}, u32[]{:S(2)}, u32[]{:S(2)}) collective-permute-start(bf16[36,36,128]{2,1,0:T(8,128)(2,1)S(1)} %collective-permute-done.12), channel_id=1, source_target_pairs={{0,128},{128,0},{256,384},{384,256},{1,129},{129,1},{257,385},{385... | collective-permute-start | bytes 995336 | tf_op jit(solution)/shard_map/ppermute | solution.py:314
where the time goes:
time: 141 us
  starting transfers between devices  83 us (59%)
  waiting for transfers between devices  43.1 us (31%)
  Pallas kernels  6.17 us (4%)
  local copies, waits for them, and re-layouts  4.82 us (3%)
  other arithmetic  2.72 us (2%)
    ppermute x10, starting transfers between devices, swap(): lax.ppermute(x, axis, [(i, i ^ mask) for i in range(lax.axis_size(axis))])  40.6 us
    ppermute x10, waiting for transfers between devices, swap(): lax.ppermute(x, axis, [(i, i ^ mask) for i in range(lax.axis_size(axis))])  32.6 us
    ppermute x1, starting transfers between devices, one_device(): lax.ppermute(eastward, 'tile', [(i, (i + TJ) % tiles) for i in range(tile...  15.3 us
    all_to_all x1, starting transfers between devices, one_device(): lax.all_to_all(sent, 'tile', split_axis=0, concat_axis=0, tiled=True)  14 us
    all_to_all x1, waiting for transfers between devices, one_device(): lax.all_to_all(sent, 'tile', split_axis=0, concat_axis=0, tiled=True)  10.5 us
    ppermute x1, starting transfers between devices, one_device(): lax.ppermute(westward, 'tile', [((i + TJ) % tiles, i) for i in range(tile...  6.83 us
    pallas_call x5, Pallas kernels, run(): return built(len(operands))(*operands)  6.17 us
    ppermute x1, starting transfers between devices, one_device(): from_south = lax.ppermute(northward, 'tile', steps_up)  4.99 us
  transfers between devices with their start and end apart: 15, of which 9 were waited for; matrix products, arithmetic and copies ran while one was open for 2% of the time, Pallas kernels for 4%

commit v1 on v0

--- a/solution.py
+++ b/solution.py
@@ -235,6 +235,20 @@
     edge_ref[1] = held
 
 
+def outer_lon_kernel(
+    me_ref, forcing_ref, south_ref, north_ref, west_ref, east_ref, planes_ref, between_ref, large_ref,
+    small_ref, inner_ref, rate_ref, local_ref, edge_ref, lon_ref, lat_ref, lonc_ref, latc_ref,
+    outer, zero, one, two, weights,
+):
+    outer_kernel(
+        forcing_ref, south_ref, north_ref, west_ref, east_ref, planes_ref, between_ref, large_ref,
+        small_ref, outer, zero, one, two, weights,
+    )
+    lon_kernel(
+        me_ref, inner_ref, outer, rate_ref, local_ref, edge_ref, lon_ref, lat_ref, lonc_ref, latc_ref
+    )
+
+
 def carries(received, coef_ref):
     ahead = jnp.zeros(received[0].shape[1:], jnp.float32)
     behind = ahead
@@ -277,17 +291,25 @@
     carry_ref[0], carry_ref[1] = carries((r0, r1, r2), coef_ref)
     ahead, behind = lat_ref[2][:NY], lat_ref[3][:NY]
 
-    def line(x, carry):
-        at = pl.multiple_of(x * YO, 8)
-        value = (
-            local_ref[pl.ds(at, NY), :]
-            + ahead * carry_ref[0, pl.ds(x, 1), :]
-            + behind * carry_ref[1, pl.ds(x, 1), :]
-        )
-        out_ref[x] = value.astype(jnp.bfloat16)
-        return carry
-
-    lax.fori_loop(0, NX, line, 0, unroll=2)
+    for x in range(0, NX, 2):
+        pair = [
+            local_ref[i * YO : i * YO + NY, :]
+            + ahead * carry_ref[0, i : i + 1, :]
+            + behind * carry_ref[1, i : i + 1, :]
+            for i in (x, x + 1)
+        ]
+        out_ref[x * NY : (x + 2) * NY, :] = jnp.concatenate(pair, 0).astype(jnp.bfloat16)
+
+
+def update_kernel(control_ref, factor_ref, p0, p1, p2, p3, out_ref):
+    for x in range(0, NX, 2):
+        rows = slice(x * NY, (x + 2) * NY)
+        total = factor_ref[0:1, :] * p0[rows, :].astype(jnp.float32)
+        for k, ref in enumerate((p1, p2, p3)):
+            total = total + factor_ref[k + 1 : k + 2, :] * ref[rows, :].astype(jnp.float32)
+        for i in range(2):
+            part = total[i * NY : (i + 1) * NY]
+            out_ref[x + i] = (control_ref[x + i].astype(jnp.float32) - part).astype(jnp.bfloat16)
 
 
 def call(kernel, outs, scratch=(), specs=None):
@@ -306,6 +328,10 @@
     return run
 
 
+def in_place(*arrays):
+    return [pltpu.with_memory_space_constraint(x, pltpu.MemorySpace.HBM) for x in arrays]
+
+
 def f32(*shape):
     return jax.ShapeDtypeStruct(shape, jnp.float32)
 
@@ -341,30 +367,76 @@
     return rows[: n * m].reshape(n, m, S), join_parts(rows[n * m :])[:, :w]
 
 
-def rate_rows(lon_rate, lat_rate):
-    lon = lon_rate[0].reshape(TI, 1, NX)
-    lat = lat_rate[0].reshape(1, TJ, NY)
-    shape = (TI, TJ)
-    columns = [
-        jnp.broadcast_to(lon, shape + (NX,)),
-        jnp.zeros(shape + (YO - NX,), jnp.float32),
-        jnp.broadcast_to(lat, shape + (NY,)),
-        jnp.zeros(shape + (YO - NY,), jnp.float32),
-        jnp.broadcast_to(jnp.sum(lon, 2).reshape(1, 1, TI), shape + (TI,)),
-        jnp.broadcast_to(jnp.sum(lat, 2).reshape(1, 1, TJ), shape + (TJ,)),
-        jnp.zeros(shape + (S - 2 * YO - TI - TJ,), jnp.float32),
-    ]
-    return jnp.concatenate(columns, 2).reshape(TI * TJ, S)
+def fetch_kernel(
+    lon_ref, lat_ref, cells_ref, transport_ref, reactivity_ref, out_ref, cells_out, coefs_out,
+    lon_copy, lat_copy, transport_copy, reactivity_copy, rows, arrived,
+):
+    pairs = (
+        (lon_ref, lon_copy),
+        (lat_ref, lat_copy),
+        (transport_ref, transport_copy),
+        (reactivity_ref, reactivity_copy),
+        (cells_ref, cells_out),
+    )
+    fetches = [pltpu.make_async_copy(a, b, arrived.at[i]) for i, (a, b) in enumerate(pairs)]
+    for fetch in fetches:
+        fetch.start()
+    rows[...] = jnp.zeros_like(rows)
+    for fetch in fetches[:2]:
+        fetch.wait()
+    for i in range(TI):
+        rows[i : i + 1, :NX] = lon_copy[:, i * NX : (i + 1) * NX]
+    for j in range(TJ):
+        rows[TI + j : TI + j + 1, YO : YO + NY] = lat_copy[:, j * NY : (j + 1) * NY]
+    parts, tiles = TI + TJ, TI * TJ
+    values = rows[...]
+    sums = lax.dot_general(
+        jnp.ones((8, S), jnp.float32), values, (((1,), (1,)), ((), ())),
+        precision=HIGHEST, preferred_element_type=jnp.float32,
+    )
+    part = lax.broadcasted_iota(jnp.int32, (parts, S), 0)
+    place = (lax.broadcasted_iota(jnp.int32, (parts, S), 1) == part + 2 * YO).astype(jnp.float32)
+    placed = jnp.dot(sums, place, precision=HIGHEST, preferred_element_type=jnp.float32)
+    tile = lax.broadcasted_iota(jnp.int32, (tiles, parts), 0)
+    part = lax.broadcasted_iota(jnp.int32, (tiles, parts), 1)
+    pick = ((part == tile // TJ) | (part == tile % TJ + TI)).astype(jnp.float32)
+    out_ref[...] = placed[:1] + jnp.dot(pick, values, precision=HIGHEST, preferred_element_type=jnp.float32)
+    for fetch in fetches[2:]:
+        fetch.wait()
+    for f in range(FLD - 1):
+        coefs_out[f] = transport_copy[f * NX : (f + 1) * NX, 0, :]
+    coefs_out[FLD - 1] = reactivity_copy[:, 0, :]
 
 
 def one_device(
     forcing, transport, reactivity, jacobian, pattern, lon_rate, lat_rate, vertical, step_scale, control
 ):
-    cells = forcing[0, 0]
     tile = lax.axis_index("tile")
     tiles = TI * TJ
-
-    coefs = jnp.concatenate([transport[:, 0, 0], reactivity[0, 0][None]], 0)
+    anywhere = pl.BlockSpec(memory_space=pltpu.MemorySpace.HBM)
+    sent, cells, coefs = call(
+        fetch_kernel,
+        (f32(tiles, S), jax.ShapeDtypeStruct((NX, NY, S), jnp.bfloat16), f32(FLD, NX, NY)),
+        (
+            pltpu.VMEM(lon_rate.shape, jnp.float32),
+            pltpu.VMEM(lat_rate.shape, jnp.float32),
+            pltpu.VMEM(((FLD - 1) * NX, 1, NY), jnp.float32),
+            pltpu.VMEM((NX, 1, NY), jnp.float32),
+            pltpu.VMEM((TI + TJ, S), jnp.float32),
+            pltpu.SemaphoreType.DMA((5,)),
+        ),
+        specs=[anywhere] * 5,
+    )(
+        *in_place(
+            lon_rate,
+            lat_rate,
+            forcing[0, 0],
+            transport.reshape((FLD - 1) * NX, 1, NY),
+            reactivity.reshape(NX, 1, NY),
+        )
+    )
+    rates = lax.all_to_all(sent, "tile", split_axis=0, concat_axis=0, tiled=True)
+
     northward = pack(
         jnp.swapaxes(cells[:, NY - 3 :], 0, 1),
         jnp.swapaxes(coefs[:, :, NY - 2 :], 1, 2).reshape(2 * FLD, NX),
@@ -377,10 +449,6 @@
     from_north = lax.ppermute(southward, "tile", [(b, a) for a, b in steps_up])
     south, south_coefs = unpack(from_south, 3, NX, NX)
     north, north_coefs = unpack(from_north, 3, NX, NX)
-    south_coefs, north_coefs, sent = lax.optimization_barrier(
-        (south_coefs, north_coefs, rate_rows(lon_rate, lat_rate))
-    )
-    rates = lax.all_to_all(sent, "tile", split_axis=0, concat_axis=0, tiled=True)
     south_coefs = jnp.swapaxes(south_coefs.reshape(FLD, 2, NX), 1, 2)
     north_coefs = jnp.swapaxes(north_coefs.reshape(FLD, 2, NX), 1, 2)
     tall = jnp.concatenate([south_coefs, coefs, north_coefs], 2)
@@ -392,8 +460,13 @@
 
     eastward = pack(side(slice(NX - 3, NX)), tall[:, NX - 2 :].reshape(2 * FLD, NY + 4))
     westward = pack(side(slice(0, 3)), tall[:, :2].reshape(2 * FLD, NY + 4))
-    from_west = lax.ppermute(eastward, "tile", [(i, (i + TJ) % tiles) for i in range(tiles)])
-    from_east = lax.ppermute(westward, "tile", [((i + TJ) % tiles, i) for i in range(tiles)])
+    upper = (tile // TJ) % 2 == 1
+    relayed = lax.ppermute(
+        jnp.where(upper, eastward, westward),
+        "tile",
+        [(i, (i + (2 * TJ if i // TJ % 2 else -2 * TJ)) % tiles) for i in range(tiles)],
+    )
+    halves = swap(jnp.stack([jnp.where(upper, westward, eastward), relayed]), "tile", TJ)
     inner, between, large, small = call(
         inner_kernel,
         (
@@ -410,8 +483,10 @@
             pltpu.VMEM((S, S), jnp.float32),
             pltpu.SemaphoreType.DMA((2,)),
         ),
-        specs=[VMEM] * 4 + [pl.BlockSpec(memory_space=pl.ANY)] * 2,
-    )(cells, south, north, widen(tall, 0, YP - NX), pattern, jacobian[0])
+        specs=[VMEM] * 4 + [anywhere] * 2,
+    )(cells, south, north, widen(tall, 0, YP - NX), *in_place(pattern, jacobian[0]))
+    from_west = jnp.where(upper, halves[0], halves[1])
+    from_east = jnp.where(upper, halves[1], halves[0])
     west, west_coefs = unpack(from_west, 3, NY + 4, NY + 4)
     east, east_coefs = unpack(from_east, 3, NY + 4, NY + 4)
     planes = jnp.concatenate(
@@ -419,17 +494,14 @@
     )
     planes = widen(planes, 1, YP - NX - 5)
 
-    outer = call(
-        outer_kernel,
-        f32(6, YO, S),
-        tuple(pltpu.VMEM((12 * YP, S), jnp.float32) for _ in range(3))
+    local, edge, lon, lat, lon_coef, lat_coef = call(
+        outer_lon_kernel,
+        (f32(NX, YO, S), f32(2, YO, S), f32(4, YO, S), f32(4, YO, S), f32(6 * 4, S), f32(6 * 3, S)),
+        (pltpu.VMEM((6, YO, S), jnp.float32),)
+        + tuple(pltpu.VMEM((12 * YP, S), jnp.float32) for _ in range(3))
         + (pltpu.VMEM((2, FLD, 5 * YP, S), jnp.float32),),
-    )(cells, south, north, west, east, planes, between, large, small)
-    local, edge, lon, lat, lon_coef, lat_coef = call(
-        lon_kernel,
-        (f32(NX, YO, S), f32(2, YO, S), f32(4, YO, S), f32(4, YO, S), f32(6 * 4, S), f32(6 * 3, S)),
-        specs=[pl.BlockSpec(memory_space=pltpu.SMEM), VMEM, VMEM, VMEM],
-    )(tile.reshape(1), inner, outer, rates)
+        specs=[pl.BlockSpec(memory_space=pltpu.SMEM)] + [VMEM] * 11,
+    )(tile.reshape(1), cells, south, north, west, east, planes, between, large, small, inner, rates)
 
     def rounds(edge, coef, bits):
         received = []
@@ -444,12 +516,14 @@
 
     level_here = lax.axis_index("lev")
     mixing = lax.dynamic_index_in_dim(vertical, level_here, 1, keepdims=False).T
-    factors = [
-        step_scale * lax.dynamic_index_in_dim(mixing, level_here ^ mask, 0, keepdims=False)
-        for mask in range(4)
-    ]
+    factors = jnp.stack(
+        [
+            step_scale * lax.dynamic_index_in_dim(mixing, level_here ^ mask, 0, keepdims=False)
+            for mask in range(4)
+        ]
+    )
     received = rounds(edge, lon_coef, LON_MASKS)
-    received[0], *factors = lax.optimization_barrier((received[0], *factors))
+    received[0], factors = lax.optimization_barrier((received[0], factors))
     local, edge = call(
         lat_kernel,
         (f32(NX * YO, S), f32(2, YO, S)),
@@ -457,17 +531,16 @@
     )(local, *received, lon_coef, lon, lat)
     filtered = call(
         finish_kernel,
-        jax.ShapeDtypeStruct((NX, NY, S), jnp.bfloat16),
+        jax.ShapeDtypeStruct((NX * NY, S), jnp.bfloat16),
         (pltpu.VMEM((2, YO, S), jnp.float32),),
     )(local, *rounds(edge, lat_coef, LAT_MASKS), lat_coef, lat)
 
     levels = [filtered, swap(filtered, "lev", 1), swap(filtered, "lev", 2)]
     levels.append(swap(levels[2], "lev", 1))
-    increment = jnp.zeros((NX, NY, S), jnp.float32)
-    for factor, plane in zip(factors, levels):
-        increment = increment + factor * plane.astype(jnp.float32)
-    updated = control[0, 0].astype(jnp.float32) - increment
-    return updated.astype(jnp.bfloat16)[None, None]
+    updated = call(update_kernel, jax.ShapeDtypeStruct((NX, NY, S), jnp.bfloat16))(
+        control[0, 0], factors, *levels
+    )
+    return updated[None, None]
 
 
 def solution(mesh):

time: 141 us -> 140 us (level)
  waiting for transfers between devices: 43.1 us -> 48.5 us
  starting transfers between devices: 83 us -> 78.7 us
  local copies, waits for them, and re-layouts: 4.82 us -> 0.92 us
  Pallas kernels: 6.17 us -> 9.02 us
    ppermute x10 -> x11, starting transfers between devices: 40.6 us -> 56.3 us  [swap(): lax.ppermute(x, axis, [(i, i ^ mask) for i in range(lax.axis_size(axis))])]
    ppermute x2 -> x1, starting transfers between devices: 22.1 us -> 7.1 us  [one_device(): lax.ppermute(jnp.where(upper, eastward, westward), 'tile', [(i, (i + (2 *...]
    all_to_all x1, starting transfers between devices: 14 us -> 9.63 us  [one_device(): lax.all_to_all(sent, 'tile', split_axis=0, concat_axis=0, tiled=True)]
    ppermute x1, waiting for transfers between devices: 0.01 us -> 3.34 us  [one_device(): from_north = lax.ppermute(southward, 'tile', [(b, a) for a, b in steps_up])]
    unnamed x18 -> x4, local copies, waits for them, and re-layouts: 2.9 us -> 0.01 us
    pallas_call x5 -> x6, Pallas kernels: 6.17 us -> 9.02 us  [run(): return built(len(operands))(*operands)]
    ppermute x10 -> x11, waiting for transfers between devices: 32.6 us -> 32.8 us  [swap(): lax.ppermute(x, axis, [(i, i ^ mask) for i in range(lax.axis_size(axis))])]
  transfers between devices with their start and end apart: 15 -> 15, of which waited for: 9 -> 11; matrix products, arithmetic and copies ran while one was open for 2% -> 1% of each run, Pallas kernels for 4% -> 3%
where the time goes in v1:
time: 140 us; the launch traced here: 139 us
  starting transfers between devices  78.7 us (56%)
  waiting for transfers between devices  48.5 us (35%)
  Pallas kernels  9.02 us (6%)
  other arithmetic  1.45 us (1%)
    ppermute x11, starting transfers between devices, swap(): lax.ppermute(x, axis, [(i, i ^ mask) for i in range(lax.axis_size(axis))])  56.3 us
    ppermute x11, waiting for transfers between devices, swap(): lax.ppermute(x, axis, [(i, i ^ mask) for i in range(lax.axis_size(axis))])  32.8 us
    all_to_all x1, waiting for transfers between devices, one_device(): lax.all_to_all(sent, 'tile', split_axis=0, concat_axis=0, tiled=True)  11.4 us
    all_to_all x1, starting transfers between devices, one_device(): lax.all_to_all(sent, 'tile', split_axis=0, concat_axis=0, tiled=True)  9.63 us
    pallas_call x6, Pallas kernels, run(): return built(len(operands))(*operands)  9.02 us
    ppermute x1, starting transfers between devices, one_device(): lax.ppermute(jnp.where(upper, eastward, westward), 'tile', [(i, (i + (2 *...  7.1 us
    ppermute x1, starting transfers between devices, one_device(): from_south = lax.ppermute(northward, 'tile', steps_up)  4.36 us
    ppermute x1, waiting for transfers between devices, one_device(): from_north = lax.ppermute(southward, 'tile', [(b, a) for a, b in steps_up])  3.34 us
  transfers between devices with their start and end apart: 15, of which 11 were waited for; matrix products, arithmetic and copies ran while one was open for 1% of the time, Pallas kernels for 3%

profile of v1, /device:TPU:1, one launch (start us, length us, event | category | flops | bytes accessed | tf_op | source)
XLA Modules:
  0.0 139.2 jit_solution(11353510355897663629)
XLA Ops:
  0.0 1.8 %shard_map.100 = (f32[128,128]{1,0:T(8,128)}, bf16[36,36,128]{2,1,0:T(8,128)(2,1)S(1)}, f32[5,36,36]{2,1,0:T(8,128)S(1)}) custom-call(f32[1,576]{1,0:T(1,128)} %lon_ref.1, f32[1,288]{1,0:T(1,128)} %lat_ref.1, bf16[36,36,128]{2,1,0:T(8,128)(2,1)} %bitcast.86, f32[144,1,36]{2,1,0:T(1,128)} %bitcast.91, f32[36,1,36]{2,1,0:T(1,128)} %bitcast.96), custom_call_target="tpu_custom_call" | custom-call | tf_op jit(solution)/shard_map/pallas_call | solution.py:317
  2.2 4.4 %collective-permute-start = (bf16[138,128]{1,0:T(8,128)(2,1)S(1)}, bf16[138,128]{1,0:T(8,128)(2,1)S(1)}, u32[]{:S(2)}, u32[]{:S(2)}) collective-permute-start(bf16[138,128]{1,0:T(8,128)(2,1)S(1)} %pad_maximum_fusion.2), channel_id=1, source_target_pairs={{0,1},{1,2},{2,3},{3,4},{4,5},{5,6},{6,7},{8,9},{9,10},{10,11},{11... | collective-permute-start | bytes 105992 | tf_op jit(solution)/shard_map/ppermute | solution.py:448
  8.3 3.3 %collective-permute-done.1 = bf16[138,128]{1,0:T(8,128)(2,1)S(1)} collective-permute-done((bf16[138,128]{1,0:T(8,128)(2,1)S(1)}, bf16[138,128]{1,0:T(8,128)(2,1)S(1)}, u32[]{:S(2)}, u32[]{:S(2)}) %collective-permute-start.1) | collective-permute-done | bytes 35360 | tf_op jit(solution)/shard_map/ppermute | solution.py:449
  12.2 7.1 %collective-permute-start.2 = (bf16[150,128]{1,0:T(8,128)(2,1)S(1)}, bf16[150,128]{1,0:T(8,128)(2,1)S(1)}, u32[]{:S(2)}, u32[]{:S(2)}) collective-permute-start(bf16[150,128]{1,0:T(8,128)(2,1)S(1)} %maximum_select_fusion.1), channel_id=1, source_target_pairs={{0,112},{1,113},{2,114},{3,115},{4,116},{5,117},{6,118},{7,119},{8... | collective-permute-start | bytes 115208 | tf_op jit(solution)/shard_map/ppermute | solution.py:464
  20.4 14.7 %collective-permute-start.3 = (bf16[2,150,128]{2,1,0:T(8,128)(2,1)S(1)}, bf16[2,150,128]{2,1,0:T(8,128)(2,1)S(1)}, u32[]{:S(2)}, u32[]{:S(2)}) collective-permute-start(bf16[2,150,128]{2,1,0:T(8,128)(2,1)S(1)} %pad_maximum_fusion.1), channel_id=1, source_target_pairs={{0,8},{1,9},{2,10},{3,11},{4,12},{5,13},{6,14},{7,15},{8,0},{9,1},... | collective-permute-start | bytes 230408 | tf_op jit(solution)/shard_map/ppermute | solution.py:340
  35.1 9.6 %all-to-all-start = ((f32[128,1,128]{2,1,0:T(1,128)}), f32[128,1,128]{2,1,0:T(1,128)S(1)}, u32[]{:S(2)}, u32[]{:S(2)}) async-start(f32[128,1,128]{2,1,0:T(1,128)} %bitcast.28), calls=%async_computation | async-start | bytes 131072 | tf_op jit(solution)/shard_map/all_to_all | solution.py:438
  44.8 4.1 %shard_map.101 = (f32[30,40,128]{2,1,0:T(8,128)S(1)}, f32[8,48,128]{2,1,0:T(8,128)S(1)}, bf16[256,256]{1,0:T(8,128)(2,1)S(1)}, bf16[256,128]{1,0:T(8,128)(2,1)S(1)}) custom-call(bf16[36,36,128]{2,1,0:T(8,128)(2,1)S(1)} %get-tuple-element.22.forcing_ref, bf16[3,36,128]{2,1,0:T(8,128)(2,1)S(1)} %reshape.211.south_ref, ...), custom_call_target="tpu_custom_call" | custom-call | tf_op jit(solution)/shard_map/pallas_call | solution.py:317
  49.2 11.4 %all-to-all-done = f32[128,1,128]{2,1,0:T(1,128)S(1)} async-done(((f32[128,1,128]{2,1,0:T(1,128)}), f32[128,1,128]{2,1,0:T(1,128)S(1)}, u32[]{:S(2)}, u32[]{:S(2)}) %all-to-all-start) | async-done | bytes 65568 | tf_op jit(solution)/shard_map/all_to_all | solution.py:438
  62.0 2.3 %collective-permute-start.4 = (f32[2,40,128]{2,1,0:T(8,128)S(1)}, f32[2,40,128]{2,1,0:T(8,128)S(1)}, u32[]{:S(2)}, u32[]{:S(2)}) collective-permute-start(f32[2,40,128]{2,1,0:T(8,128)S(1)} %get-tuple-element.29), channel_id=1, source_target_pairs={{0,8},{1,9},{2,10},{3,11},{4,12},{5,13},{6,14},{7,15},{8,0},{9,1},... | collective-permute-start | bytes 122888 | tf_op jit(solution)/shard_map/ppermute | solution.py:340
  64.3 11.2 %collective-permute-done.4.r0 = f32[2,40,128]{2,1,0:T(8,128)S(1)} collective-permute-done((f32[2,40,128]{2,1,0:T(8,128)S(1)}, f32[2,40,128]{2,1,0:T(8,128)S(1)}, u32[]{:S(2)}, u32[]{:S(2)}) %collective-permute-start.4) | collective-permute-done | bytes 40992 | tf_op jit(solution)/shard_map/ppermute | solution.py:340
  75.5 2.3 %collective-permute-start.5 = (f32[2,40,128]{2,1,0:T(8,128)S(1)}, f32[2,40,128]{2,1,0:T(8,128)S(1)}, u32[]{:S(2)}, u32[]{:S(2)}) collective-permute-start(f32[2,40,128]{2,1,0:T(8,128)S(1)} %multiply_add_fusion.4), channel_id=1, source_target_pairs={{0,16},{1,17},{2,18},{3,19},{4,20},{5,21},{6,22},{7,23},{8,24},{9,... | collective-permute-start | bytes 122888 | tf_op jit(solution)/shard_map/ppermute | solution.py:340
  77.9 3.9 %collective-permute-done.5.r1 = f32[2,40,128]{2,1,0:T(8,128)S(1)} collective-permute-done((f32[2,40,128]{2,1,0:T(8,128)S(1)}, f32[2,40,128]{2,1,0:T(8,128)S(1)}, u32[]{:S(2)}, u32[]{:S(2)}) %collective-permute-start.5) | collective-permute-done | bytes 40992 | tf_op jit(solution)/shard_map/ppermute | solution.py:340
  81.8 2.4 %collective-permute-start.6 = (f32[2,40,128]{2,1,0:T(8,128)S(1)}, f32[2,40,128]{2,1,0:T(8,128)S(1)}, u32[]{:S(2)}, u32[]{:S(2)}) collective-permute-start(f32[2,40,128]{2,1,0:T(8,128)S(1)} %multiply_add_fusion.3), channel_id=1, source_target_pairs={{0,32},{1,33},{2,34},{3,35},{4,36},{5,37},{6,38},{7,39},{8,40},{9,... | collective-permute-start | bytes 122888 | tf_op jit(solution)/shard_map/ppermute | solution.py:340
  86.6 2.3 %collective-permute-start.7 = (f32[2,40,128]{2,1,0:T(8,128)S(1)}, f32[2,40,128]{2,1,0:T(8,128)S(1)}, u32[]{:S(2)}, u32[]{:S(2)}) collective-permute-start(f32[2,40,128]{2,1,0:T(8,128)S(1)} %multiply_add_fusion.2), channel_id=1, source_target_pairs={{0,64},{1,65},{2,66},{3,67},{4,68},{5,69},{6,70},{7,71},{8,72},{9,... | collective-permute-start | bytes 122888 | tf_op jit(solution)/shard_map/ppermute | solution.py:340
  88.9 3.9 %collective-permute-done.7.r3 = f32[2,40,128]{2,1,0:T(8,128)S(1)} collective-permute-done((f32[2,40,128]{2,1,0:T(8,128)S(1)}, f32[2,40,128]{2,1,0:T(8,128)S(1)}, u32[]{:S(2)}, u32[]{:S(2)}) %collective-permute-start.7) | collective-permute-done | bytes 40992 | tf_op jit(solution)/shard_map/ppermute | solution.py:340
  93.3 3.1 %collective-permute-start.8 = (f32[2,40,128]{2,1,0:T(8,128)S(1)}, f32[2,40,128]{2,1,0:T(8,128)S(1)}, u32[]{:S(2)}, u32[]{:S(2)}) collective-permute-start(f32[2,40,128]{2,1,0:T(8,128)S(1)} %get-tuple-element.37), channel_id=1, source_target_pairs={{0,1},{1,0},{2,3},{3,2},{4,5},{5,4},{6,7},{7,6},{8,9},{9,8},{10,11... | collective-permute-start | bytes 122888 | tf_op jit(solution)/shard_map/ppermute | solution.py:340
  96.5 1.6 %collective-permute-done.8.r0 = f32[2,40,128]{2,1,0:T(8,128)S(1)} collective-permute-done((f32[2,40,128]{2,1,0:T(8,128)S(1)}, f32[2,40,128]{2,1,0:T(8,128)S(1)}, u32[]{:S(2)}, u32[]{:S(2)}) %collective-permute-start.8) | collective-permute-done | bytes 40992 | tf_op jit(solution)/shard_map/ppermute | solution.py:340
  98.1 2.3 %collective-permute-start.9 = (f32[2,40,128]{2,1,0:T(8,128)S(1)}, f32[2,40,128]{2,1,0:T(8,128)S(1)}, u32[]{:S(2)}, u32[]{:S(2)}) collective-permute-start(f32[2,40,128]{2,1,0:T(8,128)S(1)} %multiply_add_fusion.1), channel_id=1, source_target_pairs={{0,2},{1,3},{2,0},{3,1},{4,6},{5,7},{6,4},{7,5},{8,10},{9,11},{10,... | collective-permute-start | bytes 122888 | tf_op jit(solution)/shard_map/ppermute | solution.py:340
  100.4 3.3 %collective-permute-done.9.r1 = f32[2,40,128]{2,1,0:T(8,128)S(1)} collective-permute-done((f32[2,40,128]{2,1,0:T(8,128)S(1)}, f32[2,40,128]{2,1,0:T(8,128)S(1)}, u32[]{:S(2)}, u32[]{:S(2)}) %collective-permute-start.9) | collective-permute-done | bytes 40992 | tf_op jit(solution)/shard_map/ppermute | solution.py:340
  103.7 2.9 %collective-permute-start.10 = (f32[2,40,128]{2,1,0:T(8,128)S(1)}, f32[2,40,128]{2,1,0:T(8,128)S(1)}, u32[]{:S(2)}, u32[]{:S(2)}) collective-permute-start(f32[2,40,128]{2,1,0:T(8,128)S(1)} %multiply_add_fusion), channel_id=1, source_target_pairs={{0,4},{1,5},{2,6},{3,7},{4,0},{5,1},{6,2},{7,3},{8,12},{9,13},{10,... | collective-permute-start | bytes 122888 | tf_op jit(solution)/shard_map/ppermute | solution.py:340
  106.6 6.2 %collective-permute-done.10.r2 = f32[2,40,128]{2,1,0:T(8,128)S(1)} collective-permute-done((f32[2,40,128]{2,1,0:T(8,128)S(1)}, f32[2,40,128]{2,1,0:T(8,128)S(1)}, u32[]{:S(2)}, u32[]{:S(2)}) %collective-permute-start.10) | collective-permute-done | bytes 40992 | tf_op jit(solution)/shard_map/ppermute | solution.py:340
  113.0 2.2 %collective-permute-start.12 = (bf16[1296,128]{1,0:T(8,128)(2,1)S(1)}, bf16[1296,128]{1,0:T(8,128)(2,1)S(1)}, u32[]{:S(2)}, u32[]{:S(2)}) collective-permute-start(bf16[1296,128]{1,0:T(8,128)(2,1)S(1)} %shard_map.104.p0), channel_id=1, source_target_pairs={{0,256},{128,384},{256,0},{384,128},{1,257},{129,385},{257,1},{385... | collective-permute-start | bytes 995336 | tf_op jit(solution)/shard_map/ppermute | solution.py:340
  115.2 15.2 %collective-permute-start.11 = (bf16[1296,128]{1,0:T(8,128)(2,1)S(1)}, bf16[1296,128]{1,0:T(8,128)(2,1)S(1)}, u32[]{:S(2)}, u32[]{:S(2)}) collective-permute-start(bf16[1296,128]{1,0:T(8,128)(2,1)S(1)} %shard_map.104.p0), channel_id=1, source_target_pairs={{0,128},{128,0},{256,384},{384,256},{1,129},{129,1},{257,385},{385... | collective-permute-start | bytes 995336 | tf_op jit(solution)/shard_map/ppermute | solution.py:340
  130.4 6.5 %collective-permute-start.13 = (bf16[1296,128]{1,0:T(8,128)(2,1)S(1)}, bf16[1296,128]{1,0:T(8,128)(2,1)S(1)}, u32[]{:S(2)}, u32[]{:S(2)}) collective-permute-start(bf16[1296,128]{1,0:T(8,128)(2,1)S(1)} %collective-permute-done.12.p2), channel_id=1, source_target_pairs={{0,128},{128,0},{256,384},{384,256},{1,129},{129,1},{257,385},{385... | collective-permute-start | bytes 995336 | tf_op jit(solution)/shard_map/ppermute | solution.py:340
  (82 shorter events, 10.5 us)
Async XLA Ops:
  2.2 5.9 %collective-permute-start = (bf16[138,128]{1,0:T(8,128)(2,1)S(1)}, bf16[138,128]{1,0:T(8,128)(2,1)S(1)}, u32[]{:S(2)}, u32[]{:S(2)}) collective-permute-start(bf16[138,128]{1,0:T(8,128)(2,1)S(1)} %pad_maximum_fusion.2), channel_id=1, source_target_pairs={{0,1},{1,2},{2,3},{3,4},{4,5},{5,6},{6,7},{8,9},{9,10},{10,11},{11... | collective-permute-start | bytes 105992 | tf_op jit(solution)/shard_map/ppermute | solution.py:448
  6.7 4.9 %collective-permute-start.1 = (bf16[138,128]{1,0:T(8,128)(2,1)S(1)}, bf16[138,128]{1,0:T(8,128)(2,1)S(1)}, u32[]{:S(2)}, u32[]{:S(2)}) collective-permute-start(bf16[138,128]{1,0:T(8,128)(2,1)S(1)} %pad_maximum_fusion.3), channel_id=1, source_target_pairs={{1,0},{2,1},{3,2},{4,3},{5,4},{6,5},{7,6},{9,8},{10,9},{11,10},{12... | collective-permute-start | bytes 105992 | tf_op jit(solution)/shard_map/ppermute | solution.py:449
  12.2 8.2 %collective-permute-start.2 = (bf16[150,128]{1,0:T(8,128)(2,1)S(1)}, bf16[150,128]{1,0:T(8,128)(2,1)S(1)}, u32[]{:S(2)}, u32[]{:S(2)}) collective-permute-start(bf16[150,128]{1,0:T(8,128)(2,1)S(1)} %maximum_select_fusion.1), channel_id=1, source_target_pairs={{0,112},{1,113},{2,114},{3,115},{4,116},{5,117},{6,118},{7,119},{8... | collective-permute-start | bytes 115208 | tf_op jit(solution)/shard_map/ppermute | solution.py:464
  20.4 28.5 %collective-permute-start.3 = (bf16[2,150,128]{2,1,0:T(8,128)(2,1)S(1)}, bf16[2,150,128]{2,1,0:T(8,128)(2,1)S(1)}, u32[]{:S(2)}, u32[]{:S(2)}) collective-permute-start(bf16[2,150,128]{2,1,0:T(8,128)(2,1)S(1)} %pad_maximum_fusion.1), channel_id=1, source_target_pairs={{0,8},{1,9},{2,10},{3,11},{4,12},{5,13},{6,14},{7,15},{8,0},{9,1},... | collective-permute-start | bytes 230408 | tf_op jit(solution)/shard_map/ppermute | solution.py:340
  35.1 25.5 %all-to-all-start = ((f32[128,1,128]{2,1,0:T(1,128)}), f32[128,1,128]{2,1,0:T(1,128)S(1)}, u32[]{:S(2)}, u32[]{:S(2)}) async-start(f32[128,1,128]{2,1,0:T(1,128)} %bitcast.28), calls=%async_computation | async-start | bytes 131072 | tf_op jit(solution)/shard_map/all_to_all | solution.py:438
  62.0 13.5 %collective-permute-start.4 = (f32[2,40,128]{2,1,0:T(8,128)S(1)}, f32[2,40,128]{2,1,0:T(8,128)S(1)}, u32[]{:S(2)}, u32[]{:S(2)}) collective-permute-start(f32[2,40,128]{2,1,0:T(8,128)S(1)} %get-tuple-element.29), channel_id=1, source_target_pairs={{0,8},{1,9},{2,10},{3,11},{4,12},{5,13},{6,14},{7,15},{8,0},{9,1},... | collective-permute-start | bytes 122888 | tf_op jit(solution)/shard_map/ppermute | solution.py:340
  75.5 6.3 %collective-permute-start.5 = (f32[2,40,128]{2,1,0:T(8,128)S(1)}, f32[2,40,128]{2,1,0:T(8,128)S(1)}, u32[]{:S(2)}, u32[]{:S(2)}) collective-permute-start(f32[2,40,128]{2,1,0:T(8,128)S(1)} %multiply_add_fusion.4), channel_id=1, source_target_pairs={{0,16},{1,17},{2,18},{3,19},{4,20},{5,21},{6,22},{7,23},{8,24},{9,... | collective-permute-start | bytes 122888 | tf_op jit(solution)/shard_map/ppermute | solution.py:340
  81.8 2.4 %copy-start.1 = (f32[128]{0:T(128)S(1)}, f32[128]{0:T(128)}, u32[]{:S(2)}) copy-start(f32[128]{0:T(128)} %param.18) | copy-start | bytes 1540
  81.8 4.7 %collective-permute-start.6 = (f32[2,40,128]{2,1,0:T(8,128)S(1)}, f32[2,40,128]{2,1,0:T(8,128)S(1)}, u32[]{:S(2)}, u32[]{:S(2)}) collective-permute-start(f32[2,40,128]{2,1,0:T(8,128)S(1)} %multiply_add_fusion.3), channel_id=1, source_target_pairs={{0,32},{1,33},{2,34},{3,35},{4,36},{5,37},{6,38},{7,39},{8,40},{9,... | collective-permute-start | bytes 122888 | tf_op jit(solution)/shard_map/ppermute | solution.py:340
  86.6 6.3 %collective-permute-start.7 = (f32[2,40,128]{2,1,0:T(8,128)S(1)}, f32[2,40,128]{2,1,0:T(8,128)S(1)}, u32[]{:S(2)}, u32[]{:S(2)}) collective-permute-start(f32[2,40,128]{2,1,0:T(8,128)S(1)} %multiply_add_fusion.2), channel_id=1, source_target_pairs={{0,64},{1,65},{2,66},{3,67},{4,68},{5,69},{6,70},{7,71},{8,72},{9,... | collective-permute-start | bytes 122888 | tf_op jit(solution)/shard_map/ppermute | solution.py:340
  93.3 4.7 %collective-permute-start.8 = (f32[2,40,128]{2,1,0:T(8,128)S(1)}, f32[2,40,128]{2,1,0:T(8,128)S(1)}, u32[]{:S(2)}, u32[]{:S(2)}) collective-permute-start(f32[2,40,128]{2,1,0:T(8,128)S(1)} %get-tuple-element.37), channel_id=1, source_target_pairs={{0,1},{1,0},{2,3},{3,2},{4,5},{5,4},{6,7},{7,6},{8,9},{9,8},{10,11... | collective-permute-start | bytes 122888 | tf_op jit(solution)/shard_map/ppermute | solution.py:340
  98.1 5.6 %collective-permute-start.9 = (f32[2,40,128]{2,1,0:T(8,128)S(1)}, f32[2,40,128]{2,1,0:T(8,128)S(1)}, u32[]{:S(2)}, u32[]{:S(2)}) collective-permute-start(f32[2,40,128]{2,1,0:T(8,128)S(1)} %multiply_add_fusion.1), channel_id=1, source_target_pairs={{0,2},{1,3},{2,0},{3,1},{4,6},{5,7},{6,4},{7,5},{8,10},{9,11},{10,... | collective-permute-start | bytes 122888 | tf_op jit(solution)/shard_map/ppermute | solution.py:340
  103.7 9.1 %collective-permute-start.10 = (f32[2,40,128]{2,1,0:T(8,128)S(1)}, f32[2,40,128]{2,1,0:T(8,128)S(1)}, u32[]{:S(2)}, u32[]{:S(2)}) collective-permute-start(f32[2,40,128]{2,1,0:T(8,128)S(1)} %multiply_add_fusion), channel_id=1, source_target_pairs={{0,4},{1,5},{2,6},{3,7},{4,0},{5,1},{6,2},{7,3},{8,12},{9,13},{10,... | collective-permute-start | bytes 122888 | tf_op jit(solution)/shard_map/ppermute | solution.py:340
  112.8 25.3 %copy-start = (bf16[1,1,36,36,128]{4,3,2,1,0:T(8,128)(2,1)S(1)}, bf16[1,1,36,36,128]{4,3,2,1,0:T(8,128)(2,1)}, u32[]{:S(2)}) copy-start(bf16[1,1,36,36,128]{4,3,2,1,0:T(8,128)(2,1)} %param.19) | copy-start | bytes 995332
  113.0 17.4 %collective-permute-start.12 = (bf16[1296,128]{1,0:T(8,128)(2,1)S(1)}, bf16[1296,128]{1,0:T(8,128)(2,1)S(1)}, u32[]{:S(2)}, u32[]{:S(2)}) collective-permute-start(bf16[1296,128]{1,0:T(8,128)(2,1)S(1)} %shard_map.104.p0), channel_id=1, source_target_pairs={{0,256},{128,384},{256,0},{384,128},{1,257},{129,385},{257,1},{385... | collective-permute-start | bytes 995336 | tf_op jit(solution)/shard_map/ppermute | solution.py:340
  115.2 21.7 %collective-permute-start.11 = (bf16[1296,128]{1,0:T(8,128)(2,1)S(1)}, bf16[1296,128]{1,0:T(8,128)(2,1)S(1)}, u32[]{:S(2)}, u32[]{:S(2)}) collective-permute-start(bf16[1296,128]{1,0:T(8,128)(2,1)S(1)} %shard_map.104.p0), channel_id=1, source_target_pairs={{0,128},{128,0},{256,384},{384,256},{1,129},{129,1},{257,385},{385... | collective-permute-start | bytes 995336 | tf_op jit(solution)/shard_map/ppermute | solution.py:340
  130.4 7.8 %collective-permute-start.13 = (bf16[1296,128]{1,0:T(8,128)(2,1)S(1)}, bf16[1296,128]{1,0:T(8,128)(2,1)S(1)}, u32[]{:S(2)}, u32[]{:S(2)}) collective-permute-start(bf16[1296,128]{1,0:T(8,128)(2,1)S(1)} %collective-permute-done.12.p2), channel_id=1, source_target_pairs={{0,128},{128,0},{256,384},{384,256},{1,129},{129,1},{257,385},{385... | collective-permute-start | bytes 995336 | tf_op jit(solution)/shard_map/ppermute | solution.py:340

commit v2 on v1

--- a/solution.py
+++ b/solution.py
@@ -197,9 +197,7 @@
     return high, middle, (rest - middle.astype(jnp.float32)).astype(jnp.bfloat16)
 
 
-def lon_kernel(
-    me_ref, inner_ref, outer_ref, rate_ref, local_ref, edge_ref, lon_ref, lat_ref, lonc_ref, latc_ref
-):
+def tables_kernel(me_ref, rate_ref, lon_ref, lat_ref, lonc_ref, latc_ref):
     fields = rate_ref[...].T
     row = lax.broadcasted_iota(jnp.int32, (YO, YO), 0)
     col = lax.broadcasted_iota(jnp.int32, (YO, YO), 1)
@@ -217,6 +215,8 @@
     lonc_ref[...] = round_factors(me_ref[0] // TJ, fields[2 * YO : 2 * YO + TI], len(LON_MASKS))
     latc_ref[...] = round_factors(me_ref[0] % TJ, fields[2 * YO + TI : 2 * YO + TI + TJ], len(LAT_MASKS))
 
+
+def lon_kernel(inner_ref, outer_ref, lon_ref, local_ref, edge_ref):
     def gradient(x):
         if x < 3:
             return outer_ref[x]
@@ -236,17 +236,14 @@
 
 
 def outer_lon_kernel(
-    me_ref, forcing_ref, south_ref, north_ref, west_ref, east_ref, planes_ref, between_ref, large_ref,
-    small_ref, inner_ref, rate_ref, local_ref, edge_ref, lon_ref, lat_ref, lonc_ref, latc_ref,
-    outer, zero, one, two, weights,
+    forcing_ref, south_ref, north_ref, west_ref, east_ref, planes_ref, between_ref, large_ref,
+    small_ref, inner_ref, lon_ref, local_ref, edge_ref, outer, zero, one, two, weights,
 ):
     outer_kernel(
         forcing_ref, south_ref, north_ref, west_ref, east_ref, planes_ref, between_ref, large_ref,
         small_ref, outer, zero, one, two, weights,
     )
-    lon_kernel(
-        me_ref, inner_ref, outer, rate_ref, local_ref, edge_ref, lon_ref, lat_ref, lonc_ref, latc_ref
-    )
+    lon_kernel(inner_ref, outer, lon_ref, local_ref, edge_ref)
 
 
 def carries(received, coef_ref):
@@ -368,26 +365,32 @@
 
 
 def fetch_kernel(
-    lon_ref, lat_ref, cells_ref, transport_ref, reactivity_ref, out_ref, cells_out, coefs_out,
-    lon_copy, lat_copy, transport_copy, reactivity_copy, rows, arrived,
+    lon_ref, lat_ref, cells_ref, transport_ref, reactivity_ref, lon_out, lat_out, cells_out, coefs_out,
+    transport_copy, reactivity_copy, arrived,
 ):
     pairs = (
-        (lon_ref, lon_copy),
-        (lat_ref, lat_copy),
-        (transport_ref, transport_copy),
-        (reactivity_ref, reactivity_copy),
+        (transport_ref, transport_copy.at[: (FLD - 1) * NX]),
+        (reactivity_ref, reactivity_copy.at[:NX]),
         (cells_ref, cells_out),
+        (lon_ref, lon_out),
+        (lat_ref, lat_out),
     )
     fetches = [pltpu.make_async_copy(a, b, arrived.at[i]) for i, (a, b) in enumerate(pairs)]
     for fetch in fetches:
         fetch.start()
+    for fetch in fetches:
+        fetch.wait()
+    for f in range(FLD - 1):
+        coefs_out[f] = transport_copy[f * NX : (f + 1) * NX, 0, :]
+    coefs_out[FLD - 1] = reactivity_copy[:NX, 0, :]
+
+
+def rows_kernel(lon_ref, lat_ref, out_ref, rows):
     rows[...] = jnp.zeros_like(rows)
-    for fetch in fetches[:2]:
-        fetch.wait()
     for i in range(TI):
-        rows[i : i + 1, :NX] = lon_copy[:, i * NX : (i + 1) * NX]
+        rows[i : i + 1, :NX] = lon_ref[:, i * NX : (i + 1) * NX]
     for j in range(TJ):
-        rows[TI + j : TI + j + 1, YO : YO + NY] = lat_copy[:, j * NY : (j + 1) * NY]
+        rows[TI + j : TI + j + 1, YO : YO + NY] = lat_ref[:, j * NY : (j + 1) * NY]
     parts, tiles = TI + TJ, TI * TJ
     values = rows[...]
     sums = lax.dot_general(
@@ -401,11 +404,6 @@
     part = lax.broadcasted_iota(jnp.int32, (tiles, parts), 1)
     pick = ((part == tile // TJ) | (part == tile % TJ + TI)).astype(jnp.float32)
     out_ref[...] = placed[:1] + jnp.dot(pick, values, precision=HIGHEST, preferred_element_type=jnp.float32)
-    for fetch in fetches[2:]:
-        fetch.wait()
-    for f in range(FLD - 1):
-        coefs_out[f] = transport_copy[f * NX : (f + 1) * NX, 0, :]
-    coefs_out[FLD - 1] = reactivity_copy[:, 0, :]
 
 
 def one_device(
@@ -414,15 +412,17 @@
     tile = lax.axis_index("tile")
     tiles = TI * TJ
     anywhere = pl.BlockSpec(memory_space=pltpu.MemorySpace.HBM)
-    sent, cells, coefs = call(
+    lon_here, lat_here, cells, coefs = call(
         fetch_kernel,
-        (f32(tiles, S), jax.ShapeDtypeStruct((NX, NY, S), jnp.bfloat16), f32(FLD, NX, NY)),
         (
-            pltpu.VMEM(lon_rate.shape, jnp.float32),
-            pltpu.VMEM(lat_rate.shape, jnp.float32),
-            pltpu.VMEM(((FLD - 1) * NX, 1, NY), jnp.float32),
-            pltpu.VMEM((NX, 1, NY), jnp.float32),
-            pltpu.VMEM((TI + TJ, S), jnp.float32),
+            f32(*lon_rate.shape),
+            f32(*lat_rate.shape),
+            jax.ShapeDtypeStruct((NX, NY, S), jnp.bfloat16),
+            f32(FLD, NX, NY),
+        ),
+        (
+            pltpu.VMEM(((FLD - 1) * NX + 8, 1, NY), jnp.float32),
+            pltpu.VMEM((NX + 8, 1, NY), jnp.float32),
             pltpu.SemaphoreType.DMA((5,)),
         ),
         specs=[anywhere] * 5,
@@ -435,6 +435,7 @@
             reactivity.reshape(NX, 1, NY),
         )
     )
+    sent = call(rows_kernel, f32(tiles, S), (pltpu.VMEM((TI + TJ, S), jnp.float32),))(lon_here, lat_here)
     rates = lax.all_to_all(sent, "tile", split_axis=0, concat_axis=0, tiled=True)
 
     northward = pack(
@@ -476,8 +477,8 @@
             jax.ShapeDtypeStruct((2 * S, S), jnp.bfloat16),
         ),
         (
-            pltpu.VMEM((NX * YP, S), jnp.float32),
-            pltpu.VMEM((NX * YP, S), jnp.float32),
+            pltpu.VMEM((YO * YP, S), jnp.float32),
+            pltpu.VMEM((YO * YP, S), jnp.float32),
             pltpu.VMEM((FLD, NX * YP, S), jnp.float32),
             pltpu.VMEM(pattern.shape, pattern.dtype),
             pltpu.VMEM((S, S), jnp.float32),
@@ -494,14 +495,18 @@
     )
     planes = widen(planes, 1, YP - NX - 5)
 
-    local, edge, lon, lat, lon_coef, lat_coef = call(
+    lon, lat, lon_coef, lat_coef = call(
+        tables_kernel,
+        (f32(4, YO, S), f32(4, YO, S), f32(6 * 4, S), f32(6 * 3, S)),
+        specs=[pl.BlockSpec(memory_space=pltpu.SMEM), VMEM],
+    )(tile.reshape(1), rates)
+    local, edge = call(
         outer_lon_kernel,
-        (f32(NX, YO, S), f32(2, YO, S), f32(4, YO, S), f32(4, YO, S), f32(6 * 4, S), f32(6 * 3, S)),
+        (f32(NX, YO, S), f32(2, YO, S)),
         (pltpu.VMEM((6, YO, S), jnp.float32),)
-        + tuple(pltpu.VMEM((12 * YP, S), jnp.float32) for _ in range(3))
+        + tuple(pltpu.VMEM((16 * YP, S), jnp.float32) for _ in range(3))
         + (pltpu.VMEM((2, FLD, 5 * YP, S), jnp.float32),),
-        specs=[pl.BlockSpec(memory_space=pltpu.SMEM)] + [VMEM] * 11,
-    )(tile.reshape(1), cells, south, north, west, east, planes, between, large, small, inner, rates)
+    )(cells, south, north, west, east, planes, between, large, small, inner, lon)
 
     def rounds(edge, coef, bits):
         received = []
@@ -526,8 +531,8 @@
     received[0], factors = lax.optimization_barrier((received[0], factors))
     local, edge = call(
         lat_kernel,
-        (f32(NX * YO, S), f32(2, YO, S)),
-        (pltpu.VMEM((NX * YO, S), jnp.float32), pltpu.VMEM((NY, NX, S), jnp.float32)),
+        (f32(YO * YO, S), f32(2, YO, S)),
+        (pltpu.VMEM((YO * YO, S), jnp.float32), pltpu.VMEM((NY, NX, S), jnp.float32)),
     )(local, *received, lon_coef, lon, lat)
     filtered = call(
         finish_kernel,

time: 140 us -> 140 us (level)
    pallas_call x6 -> x8, Pallas kernels: 9.02 us -> 9.61 us  [run(): return built(len(operands))(*operands)]
  transfers between devices with their start and end apart: 15 -> 15, of which waited for: 11 -> 11; matrix products, arithmetic and copies ran while one was open for 1% -> 1% of each run, Pallas kernels for 3% -> 4%
where the time goes in v2:
time: 140 us
  starting transfers between devices  78.2 us (56%)
  waiting for transfers between devices  49 us (35%)
  Pallas kernels  9.61 us (7%)
  other arithmetic  1.45 us (1%)
    ppermute x11, starting transfers between devices, swap(): lax.ppermute(x, axis, [(i, i ^ mask) for i in range(lax.axis_size(axis))])  55.8 us
    ppermute x11, waiting for transfers between devices, swap(): lax.ppermute(x, axis, [(i, i ^ mask) for i in range(lax.axis_size(axis))])  33.3 us
    all_to_all x1, waiting for transfers between devices, one_device(): lax.all_to_all(sent, 'tile', split_axis=0, concat_axis=0, tiled=True)  11.4 us
    all_to_all x1, starting transfers between devices, one_device(): lax.all_to_all(sent, 'tile', split_axis=0, concat_axis=0, tiled=True)  9.62 us
    pallas_call x8, Pallas kernels, run(): return built(len(operands))(*operands)  9.61 us
    ppermute x1, starting transfers between devices, one_device(): lax.ppermute(jnp.where(upper, eastward, westward), 'tile', [(i, (i + (2 *...  7.1 us
    ppermute x1, starting transfers between devices, one_device(): from_south = lax.ppermute(northward, 'tile', steps_up)  4.36 us
    ppermute x1, waiting for transfers between devices, one_device(): from_north = lax.ppermute(southward, 'tile', [(b, a) for a, b in steps_up])  3.34 us
  transfers between devices with their start and end apart: 15, of which 11 were waited for; matrix products, arithmetic and copies ran while one was open for 1% of the time, Pallas kernels for 4%

profile of v2, /device:TPU:1, one launch (start us, length us, event | category | flops | bytes accessed | tf_op | source)
XLA Modules:
  0.0 139.8 jit_solution(3748082474581439143)
XLA Ops:
  1.5 4.4 %collective-permute-start = (bf16[138,128]{1,0:T(8,128)(2,1)S(1)}, bf16[138,128]{1,0:T(8,128)(2,1)S(1)}, u32[]{:S(2)}, u32[]{:S(2)}) collective-permute-start(bf16[138,128]{1,0:T(8,128)(2,1)S(1)} %pad_maximum_fusion.2), channel_id=1, source_target_pairs={{0,1},{1,2},{2,3},{3,4},{4,5},{5,6},{6,7},{8,9},{9,10},{10,11},{11... | collective-permute-start | bytes 105992 | tf_op jit(solution)/shard_map/ppermute | solution.py:449
  7.6 3.3 %collective-permute-done.1 = bf16[138,128]{1,0:T(8,128)(2,1)S(1)} collective-permute-done((bf16[138,128]{1,0:T(8,128)(2,1)S(1)}, bf16[138,128]{1,0:T(8,128)(2,1)S(1)}, u32[]{:S(2)}, u32[]{:S(2)}) %collective-permute-start.1) | collective-permute-done | bytes 35360 | tf_op jit(solution)/shard_map/ppermute | solution.py:450
  11.5 7.1 %collective-permute-start.2 = (bf16[150,128]{1,0:T(8,128)(2,1)S(1)}, bf16[150,128]{1,0:T(8,128)(2,1)S(1)}, u32[]{:S(2)}, u32[]{:S(2)}) collective-permute-start(bf16[150,128]{1,0:T(8,128)(2,1)S(1)} %maximum_select_fusion.1), channel_id=1, source_target_pairs={{0,112},{1,113},{2,114},{3,115},{4,116},{5,117},{6,118},{7,119},{8... | collective-permute-start | bytes 115208 | tf_op jit(solution)/shard_map/ppermute | solution.py:465
  19.7 14.7 %collective-permute-start.3 = (bf16[2,150,128]{2,1,0:T(8,128)(2,1)S(1)}, bf16[2,150,128]{2,1,0:T(8,128)(2,1)S(1)}, u32[]{:S(2)}, u32[]{:S(2)}) collective-permute-start(bf16[2,150,128]{2,1,0:T(8,128)(2,1)S(1)} %pad_maximum_fusion.1), channel_id=1, source_target_pairs={{0,8},{1,9},{2,10},{3,11},{4,12},{5,13},{6,14},{7,15},{8,0},{9,1},... | collective-permute-start | bytes 230408 | tf_op jit(solution)/shard_map/ppermute | solution.py:337
  35.5 9.6 %all-to-all-start = ((f32[128,1,128]{2,1,0:T(1,128)}), f32[128,1,128]{2,1,0:T(1,128)S(1)}, u32[]{:S(2)}, u32[]{:S(2)}) async-start(f32[128,1,128]{2,1,0:T(1,128)} %bitcast.28), calls=%async_computation | async-start | bytes 131072 | tf_op jit(solution)/shard_map/all_to_all | solution.py:439
  45.2 4.1 %shard_map.101 = (f32[30,40,128]{2,1,0:T(8,128)S(1)}, f32[8,48,128]{2,1,0:T(8,128)S(1)}, bf16[256,256]{1,0:T(8,128)(2,1)S(1)}, bf16[256,128]{1,0:T(8,128)(2,1)S(1)}) custom-call(bf16[36,36,128]{2,1,0:T(8,128)(2,1)S(1)} %get-tuple-element.23.forcing_ref, bf16[3,36,128]{2,1,0:T(8,128)(2,1)S(1)} %reshape.210.south_ref, ...), custom_call_target="tpu_custom_call" | custom-call | tf_op jit(solution)/shard_map/pallas_call | solution.py:314
  49.6 11.4 %all-to-all-done = f32[128,1,128]{2,1,0:T(1,128)S(1)} async-done(((f32[128,1,128]{2,1,0:T(1,128)}), f32[128,1,128]{2,1,0:T(1,128)S(1)}, u32[]{:S(2)}, u32[]{:S(2)}) %all-to-all-start) | async-done | bytes 65568 | tf_op jit(solution)/shard_map/all_to_all | solution.py:439
  62.6 2.3 %collective-permute-start.4 = (f32[2,40,128]{2,1,0:T(8,128)S(1)}, f32[2,40,128]{2,1,0:T(8,128)S(1)}, u32[]{:S(2)}, u32[]{:S(2)}) collective-permute-start(f32[2,40,128]{2,1,0:T(8,128)S(1)} %get-tuple-element.32), channel_id=1, source_target_pairs={{0,8},{1,9},{2,10},{3,11},{4,12},{5,13},{6,14},{7,15},{8,0},{9,1},... | collective-permute-start | bytes 122888 | tf_op jit(solution)/shard_map/ppermute | solution.py:337
  64.9 11.2 %collective-permute-done.4.r0 = f32[2,40,128]{2,1,0:T(8,128)S(1)} collective-permute-done((f32[2,40,128]{2,1,0:T(8,128)S(1)}, f32[2,40,128]{2,1,0:T(8,128)S(1)}, u32[]{:S(2)}, u32[]{:S(2)}) %collective-permute-start.4) | collective-permute-done | bytes 40992 | tf_op jit(solution)/shard_map/ppermute | solution.py:337
  76.1 2.3 %collective-permute-start.5 = (f32[2,40,128]{2,1,0:T(8,128)S(1)}, f32[2,40,128]{2,1,0:T(8,128)S(1)}, u32[]{:S(2)}, u32[]{:S(2)}) collective-permute-start(f32[2,40,128]{2,1,0:T(8,128)S(1)} %multiply_add_fusion.4), channel_id=1, source_target_pairs={{0,16},{1,17},{2,18},{3,19},{4,20},{5,21},{6,22},{7,23},{8,24},{9,... | collective-permute-start | bytes 122888 | tf_op jit(solution)/shard_map/ppermute | solution.py:337
  78.5 3.9 %collective-permute-done.5.r1 = f32[2,40,128]{2,1,0:T(8,128)S(1)} collective-permute-done((f32[2,40,128]{2,1,0:T(8,128)S(1)}, f32[2,40,128]{2,1,0:T(8,128)S(1)}, u32[]{:S(2)}, u32[]{:S(2)}) %collective-permute-start.5) | collective-permute-done | bytes 40992 | tf_op jit(solution)/shard_map/ppermute | solution.py:337
  82.4 2.4 %collective-permute-start.6 = (f32[2,40,128]{2,1,0:T(8,128)S(1)}, f32[2,40,128]{2,1,0:T(8,128)S(1)}, u32[]{:S(2)}, u32[]{:S(2)}) collective-permute-start(f32[2,40,128]{2,1,0:T(8,128)S(1)} %multiply_add_fusion.3), channel_id=1, source_target_pairs={{0,32},{1,33},{2,34},{3,35},{4,36},{5,37},{6,38},{7,39},{8,40},{9,... | collective-permute-start | bytes 122888 | tf_op jit(solution)/shard_map/ppermute | solution.py:337
  85.6 1.5 %collective-permute-done.6.r2 = f32[2,40,128]{2,1,0:T(8,128)S(1)} collective-permute-done((f32[2,40,128]{2,1,0:T(8,128)S(1)}, f32[2,40,128]{2,1,0:T(8,128)S(1)}, u32[]{:S(2)}, u32[]{:S(2)}) %collective-permute-start.6) | collective-permute-done | bytes 40992 | tf_op jit(solution)/shard_map/ppermute | solution.py:337
  87.1 2.3 %collective-permute-start.7 = (f32[2,40,128]{2,1,0:T(8,128)S(1)}, f32[2,40,128]{2,1,0:T(8,128)S(1)}, u32[]{:S(2)}, u32[]{:S(2)}) collective-permute-start(f32[2,40,128]{2,1,0:T(8,128)S(1)} %multiply_add_fusion.2), channel_id=1, source_target_pairs={{0,64},{1,65},{2,66},{3,67},{4,68},{5,69},{6,70},{7,71},{8,72},{9,... | collective-permute-start | bytes 122888 | tf_op jit(solution)/shard_map/ppermute | solution.py:337
  89.5 3.9 %collective-permute-done.7.r3 = f32[2,40,128]{2,1,0:T(8,128)S(1)} collective-permute-done((f32[2,40,128]{2,1,0:T(8,128)S(1)}, f32[2,40,128]{2,1,0:T(8,128)S(1)}, u32[]{:S(2)}, u32[]{:S(2)}) %collective-permute-start.7) | collective-permute-done | bytes 40992 | tf_op jit(solution)/shard_map/ppermute | solution.py:337
  93.9 3.1 %collective-permute-start.8 = (f32[2,40,128]{2,1,0:T(8,128)S(1)}, f32[2,40,128]{2,1,0:T(8,128)S(1)}, u32[]{:S(2)}, u32[]{:S(2)}) collective-permute-start(f32[2,40,128]{2,1,0:T(8,128)S(1)} %get-tuple-element.39), channel_id=1, source_target_pairs={{0,1},{1,0},{2,3},{3,2},{4,5},{5,4},{6,7},{7,6},{8,9},{9,8},{10,11... | collective-permute-start | bytes 122888 | tf_op jit(solution)/shard_map/ppermute | solution.py:337
  97.0 1.6 %collective-permute-done.8.r0 = f32[2,40,128]{2,1,0:T(8,128)S(1)} collective-permute-done((f32[2,40,128]{2,1,0:T(8,128)S(1)}, f32[2,40,128]{2,1,0:T(8,128)S(1)}, u32[]{:S(2)}, u32[]{:S(2)}) %collective-permute-start.8) | collective-permute-done | bytes 40992 | tf_op jit(solution)/shard_map/ppermute | solution.py:337
  98.7 2.3 %collective-permute-start.9 = (f32[2,40,128]{2,1,0:T(8,128)S(1)}, f32[2,40,128]{2,1,0:T(8,128)S(1)}, u32[]{:S(2)}, u32[]{:S(2)}) collective-permute-start(f32[2,40,128]{2,1,0:T(8,128)S(1)} %multiply_add_fusion.1), channel_id=1, source_target_pairs={{0,2},{1,3},{2,0},{3,1},{4,6},{5,7},{6,4},{7,5},{8,10},{9,11},{10,... | collective-permute-start | bytes 122888 | tf_op jit(solution)/shard_map/ppermute | solution.py:337
  101.0 3.3 %collective-permute-done.9.r1 = f32[2,40,128]{2,1,0:T(8,128)S(1)} collective-permute-done((f32[2,40,128]{2,1,0:T(8,128)S(1)}, f32[2,40,128]{2,1,0:T(8,128)S(1)}, u32[]{:S(2)}, u32[]{:S(2)}) %collective-permute-start.9) | collective-permute-done | bytes 40992 | tf_op jit(solution)/shard_map/ppermute | solution.py:337
  104.3 2.4 %collective-permute-start.10 = (f32[2,40,128]{2,1,0:T(8,128)S(1)}, f32[2,40,128]{2,1,0:T(8,128)S(1)}, u32[]{:S(2)}, u32[]{:S(2)}) collective-permute-start(f32[2,40,128]{2,1,0:T(8,128)S(1)} %multiply_add_fusion), channel_id=1, source_target_pairs={{0,4},{1,5},{2,6},{3,7},{4,0},{5,1},{6,2},{7,3},{8,12},{9,13},{10,... | collective-permute-start | bytes 122888 | tf_op jit(solution)/shard_map/ppermute | solution.py:337
  106.7 6.7 %collective-permute-done.10.r2 = f32[2,40,128]{2,1,0:T(8,128)S(1)} collective-permute-done((f32[2,40,128]{2,1,0:T(8,128)S(1)}, f32[2,40,128]{2,1,0:T(8,128)S(1)}, u32[]{:S(2)}, u32[]{:S(2)}) %collective-permute-start.10) | collective-permute-done | bytes 40992 | tf_op jit(solution)/shard_map/ppermute | solution.py:337
  113.6 2.2 %collective-permute-start.12 = (bf16[1296,128]{1,0:T(8,128)(2,1)S(1)}, bf16[1296,128]{1,0:T(8,128)(2,1)S(1)}, u32[]{:S(2)}, u32[]{:S(2)}) collective-permute-start(bf16[1296,128]{1,0:T(8,128)(2,1)S(1)} %shard_map.106.p0), channel_id=1, source_target_pairs={{0,256},{128,384},{256,0},{384,128},{1,257},{129,385},{257,1},{385... | collective-permute-start | bytes 995336 | tf_op jit(solution)/shard_map/ppermute | solution.py:337
  115.8 15.2 %collective-permute-start.11 = (bf16[1296,128]{1,0:T(8,128)(2,1)S(1)}, bf16[1296,128]{1,0:T(8,128)(2,1)S(1)}, u32[]{:S(2)}, u32[]{:S(2)}) collective-permute-start(bf16[1296,128]{1,0:T(8,128)(2,1)S(1)} %shard_map.106.p0), channel_id=1, source_target_pairs={{0,128},{128,0},{256,384},{384,256},{1,129},{129,1},{257,385},{385... | collective-permute-start | bytes 995336 | tf_op jit(solution)/shard_map/ppermute | solution.py:337
  131.0 6.5 %collective-permute-start.13 = (bf16[1296,128]{1,0:T(8,128)(2,1)S(1)}, bf16[1296,128]{1,0:T(8,128)(2,1)S(1)}, u32[]{:S(2)}, u32[]{:S(2)}) collective-permute-start(bf16[1296,128]{1,0:T(8,128)(2,1)S(1)} %collective-permute-done.12.p2), channel_id=1, source_target_pairs={{0,128},{128,0},{256,384},{384,256},{1,129},{129,1},{257,385},{385... | collective-permute-start | bytes 995336 | tf_op jit(solution)/shard_map/ppermute | solution.py:337
  (84 shorter events, 11.5 us)
Async XLA Ops:
  1.5 5.9 %collective-permute-start = (bf16[138,128]{1,0:T(8,128)(2,1)S(1)}, bf16[138,128]{1,0:T(8,128)(2,1)S(1)}, u32[]{:S(2)}, u32[]{:S(2)}) collective-permute-start(bf16[138,128]{1,0:T(8,128)(2,1)S(1)} %pad_maximum_fusion.2), channel_id=1, source_target_pairs={{0,1},{1,2},{2,3},{3,4},{4,5},{5,6},{6,7},{8,9},{9,10},{10,11},{11... | collective-permute-start | bytes 105992 | tf_op jit(solution)/shard_map/ppermute | solution.py:449
  6.0 4.9 %collective-permute-start.1 = (bf16[138,128]{1,0:T(8,128)(2,1)S(1)}, bf16[138,128]{1,0:T(8,128)(2,1)S(1)}, u32[]{:S(2)}, u32[]{:S(2)}) collective-permute-start(bf16[138,128]{1,0:T(8,128)(2,1)S(1)} %pad_maximum_fusion.3), channel_id=1, source_target_pairs={{1,0},{2,1},{3,2},{4,3},{5,4},{6,5},{7,6},{9,8},{10,9},{11,10},{12... | collective-permute-start | bytes 105992 | tf_op jit(solution)/shard_map/ppermute | solution.py:450
  11.5 8.2 %collective-permute-start.2 = (bf16[150,128]{1,0:T(8,128)(2,1)S(1)}, bf16[150,128]{1,0:T(8,128)(2,1)S(1)}, u32[]{:S(2)}, u32[]{:S(2)}) collective-permute-start(bf16[150,128]{1,0:T(8,128)(2,1)S(1)} %maximum_select_fusion.1), channel_id=1, source_target_pairs={{0,112},{1,113},{2,114},{3,115},{4,116},{5,117},{6,118},{7,119},{8... | collective-permute-start | bytes 115208 | tf_op jit(solution)/shard_map/ppermute | solution.py:465
  19.7 29.6 %collective-permute-start.3 = (bf16[2,150,128]{2,1,0:T(8,128)(2,1)S(1)}, bf16[2,150,128]{2,1,0:T(8,128)(2,1)S(1)}, u32[]{:S(2)}, u32[]{:S(2)}) collective-permute-start(bf16[2,150,128]{2,1,0:T(8,128)(2,1)S(1)} %pad_maximum_fusion.1), channel_id=1, source_target_pairs={{0,8},{1,9},{2,10},{3,11},{4,12},{5,13},{6,14},{7,15},{8,0},{9,1},... | collective-permute-start | bytes 230408 | tf_op jit(solution)/shard_map/ppermute | solution.py:337
  35.5 25.5 %all-to-all-start = ((f32[128,1,128]{2,1,0:T(1,128)}), f32[128,1,128]{2,1,0:T(1,128)S(1)}, u32[]{:S(2)}, u32[]{:S(2)}) async-start(f32[128,1,128]{2,1,0:T(1,128)} %bitcast.28), calls=%async_computation | async-start | bytes 131072 | tf_op jit(solution)/shard_map/all_to_all | solution.py:439
  62.6 13.5 %collective-permute-start.4 = (f32[2,40,128]{2,1,0:T(8,128)S(1)}, f32[2,40,128]{2,1,0:T(8,128)S(1)}, u32[]{:S(2)}, u32[]{:S(2)}) collective-permute-start(f32[2,40,128]{2,1,0:T(8,128)S(1)} %get-tuple-element.32), channel_id=1, source_target_pairs={{0,8},{1,9},{2,10},{3,11},{4,12},{5,13},{6,14},{7,15},{8,0},{9,1},... | collective-permute-start | bytes 122888 | tf_op jit(solution)/shard_map/ppermute | solution.py:337
  76.1 6.3 %collective-permute-start.5 = (f32[2,40,128]{2,1,0:T(8,128)S(1)}, f32[2,40,128]{2,1,0:T(8,128)S(1)}, u32[]{:S(2)}, u32[]{:S(2)}) collective-permute-start(f32[2,40,128]{2,1,0:T(8,128)S(1)} %multiply_add_fusion.4), channel_id=1, source_target_pairs={{0,16},{1,17},{2,18},{3,19},{4,20},{5,21},{6,22},{7,23},{8,24},{9,... | collective-permute-start | bytes 122888 | tf_op jit(solution)/shard_map/ppermute | solution.py:337
  82.4 2.4 %copy-start.1 = (f32[128]{0:T(128)S(1)}, f32[128]{0:T(128)}, u32[]{:S(2)}) copy-start(f32[128]{0:T(128)} %param.18) | copy-start | bytes 1540
  82.4 4.7 %collective-permute-start.6 = (f32[2,40,128]{2,1,0:T(8,128)S(1)}, f32[2,40,128]{2,1,0:T(8,128)S(1)}, u32[]{:S(2)}, u32[]{:S(2)}) collective-permute-start(f32[2,40,128]{2,1,0:T(8,128)S(1)} %multiply_add_fusion.3), channel_id=1, source_target_pairs={{0,32},{1,33},{2,34},{3,35},{4,36},{5,37},{6,38},{7,39},{8,40},{9,... | collective-permute-start | bytes 122888 | tf_op jit(solution)/shard_map/ppermute | solution.py:337
  87.1 6.3 %collective-permute-start.7 = (f32[2,40,128]{2,1,0:T(8,128)S(1)}, f32[2,40,128]{2,1,0:T(8,128)S(1)}, u32[]{:S(2)}, u32[]{:S(2)}) collective-permute-start(f32[2,40,128]{2,1,0:T(8,128)S(1)} %multiply_add_fusion.2), channel_id=1, source_target_pairs={{0,64},{1,65},{2,66},{3,67},{4,68},{5,69},{6,70},{7,71},{8,72},{9,... | collective-permute-start | bytes 122888 | tf_op jit(solution)/shard_map/ppermute | solution.py:337
  93.9 4.7 %collective-permute-start.8 = (f32[2,40,128]{2,1,0:T(8,128)S(1)}, f32[2,40,128]{2,1,0:T(8,128)S(1)}, u32[]{:S(2)}, u32[]{:S(2)}) collective-permute-start(f32[2,40,128]{2,1,0:T(8,128)S(1)} %get-tuple-element.39), channel_id=1, source_target_pairs={{0,1},{1,0},{2,3},{3,2},{4,5},{5,4},{6,7},{7,6},{8,9},{9,8},{10,11... | collective-permute-start | bytes 122888 | tf_op jit(solution)/shard_map/ppermute | solution.py:337
  98.7 5.6 %collective-permute-start.9 = (f32[2,40,128]{2,1,0:T(8,128)S(1)}, f32[2,40,128]{2,1,0:T(8,128)S(1)}, u32[]{:S(2)}, u32[]{:S(2)}) collective-permute-start(f32[2,40,128]{2,1,0:T(8,128)S(1)} %multiply_add_fusion.1), channel_id=1, source_target_pairs={{0,2},{1,3},{2,0},{3,1},{4,6},{5,7},{6,4},{7,5},{8,10},{9,11},{10,... | collective-permute-start | bytes 122888 | tf_op jit(solution)/shard_map/ppermute | solution.py:337
  104.3 9.1 %collective-permute-start.10 = (f32[2,40,128]{2,1,0:T(8,128)S(1)}, f32[2,40,128]{2,1,0:T(8,128)S(1)}, u32[]{:S(2)}, u32[]{:S(2)}) collective-permute-start(f32[2,40,128]{2,1,0:T(8,128)S(1)} %multiply_add_fusion), channel_id=1, source_target_pairs={{0,4},{1,5},{2,6},{3,7},{4,0},{5,1},{6,2},{7,3},{8,12},{9,13},{10,... | collective-permute-start | bytes 122888 | tf_op jit(solution)/shard_map/ppermute | solution.py:337
  113.4 25.3 %copy-start = (bf16[1,1,36,36,128]{4,3,2,1,0:T(8,128)(2,1)S(1)}, bf16[1,1,36,36,128]{4,3,2,1,0:T(8,128)(2,1)}, u32[]{:S(2)}) copy-start(bf16[1,1,36,36,128]{4,3,2,1,0:T(8,128)(2,1)} %param.19) | copy-start | bytes 995332
  113.6 17.4 %collective-permute-start.12 = (bf16[1296,128]{1,0:T(8,128)(2,1)S(1)}, bf16[1296,128]{1,0:T(8,128)(2,1)S(1)}, u32[]{:S(2)}, u32[]{:S(2)}) collective-permute-start(bf16[1296,128]{1,0:T(8,128)(2,1)S(1)} %shard_map.106.p0), channel_id=1, source_target_pairs={{0,256},{128,384},{256,0},{384,128},{1,257},{129,385},{257,1},{385... | collective-permute-start | bytes 995336 | tf_op jit(solution)/shard_map/ppermute | solution.py:337
  115.8 21.7 %collective-permute-start.11 = (bf16[1296,128]{1,0:T(8,128)(2,1)S(1)}, bf16[1296,128]{1,0:T(8,128)(2,1)S(1)}, u32[]{:S(2)}, u32[]{:S(2)}) collective-permute-start(bf16[1296,128]{1,0:T(8,128)(2,1)S(1)} %shard_map.106.p0), channel_id=1, source_target_pairs={{0,128},{128,0},{256,384},{384,256},{1,129},{129,1},{257,385},{385... | collective-permute-start | bytes 995336 | tf_op jit(solution)/shard_map/ppermute | solution.py:337
  131.0 7.8 %collective-permute-start.13 = (bf16[1296,128]{1,0:T(8,128)(2,1)S(1)}, bf16[1296,128]{1,0:T(8,128)(2,1)S(1)}, u32[]{:S(2)}, u32[]{:S(2)}) collective-permute-start(bf16[1296,128]{1,0:T(8,128)(2,1)S(1)} %collective-permute-done.12.p2), channel_id=1, source_target_pairs={{0,128},{128,0},{256,384},{384,256},{1,129},{129,1},{257,385},{385... | collective-permute-start | bytes 995336 | tf_op jit(solution)/shard_map/ppermute | solution.py:337

commit v3 on v2

--- a/solution.py
+++ b/solution.py
@@ -342,13 +342,12 @@
     rest = x - high
     middle = lax.reduce_precision(rest, 8, 7)
     low = rest - middle
-    return jnp.concatenate([high, middle, low], 0).astype(jnp.bfloat16)
-
-
-def join_parts(parts):
-    third = parts.shape[0] // 3
+    return jnp.concatenate([high, middle, low], 1).astype(jnp.bfloat16)
+
+
+def join_parts(parts, w):
     parts = parts.astype(jnp.float32)
-    return (parts[:third] + parts[third : 2 * third]) + parts[2 * third :]
+    return (parts[:, :w] + parts[:, w : 2 * w]) + parts[:, 2 * w : 3 * w]
 
 
 def widen(coefs, before, after):
@@ -356,12 +355,13 @@
 
 
 def pack(cells, coefs):
-    wide = jnp.pad(coefs, ((0, 0), (0, S - coefs.shape[1])))
-    return jnp.concatenate([cells.reshape(-1, S), three_parts(wide)], 0)
+    parts = three_parts(coefs)
+    wide = jnp.pad(parts, ((0, 0), (0, S - parts.shape[1])))
+    return jnp.concatenate([cells.reshape(-1, S), wide], 0)
 
 
 def unpack(rows, n, m, w):
-    return rows[: n * m].reshape(n, m, S), join_parts(rows[n * m :])[:, :w]
+    return rows[: n * m].reshape(n, m, S), join_parts(rows[n * m :], w)
 
 
 def fetch_kernel(

time: 140 us -> 142 us (1.014)
  starting transfers between devices: 78.2 us -> 82 us
  waiting for transfers between devices: 49 us -> 46.2 us
    ppermute x1, waiting for transfers between devices: 3.34 us -> 0.01 us  [one_device(): from_north = lax.ppermute(southward, 'tile', [(b, a) for a, b in steps_up])]
    all_to_all x1, starting transfers between devices: 9.62 us -> 11.9 us  [one_device(): lax.all_to_all(sent, 'tile', split_axis=0, concat_axis=0, tiled=True)]
where the time goes in v3:
time: 142 us; the launch traced here: 141 us
  starting transfers between devices  82 us (58%)
  waiting for transfers between devices  46.2 us (33%)
  Pallas kernels  9.61 us (7%)
  other arithmetic  1.92 us (1%)
    ppermute x11, starting transfers between devices, swap(): lax.ppermute(x, axis, [(i, i ^ mask) for i in range(lax.axis_size(axis))])  56.7 us
    ppermute x11, waiting for transfers between devices, swap(): lax.ppermute(x, axis, [(i, i ^ mask) for i in range(lax.axis_size(axis))])  33.3 us
    all_to_all x1, starting transfers between devices, one_device(): lax.all_to_all(sent, 'tile', split_axis=0, concat_axis=0, tiled=True)  11.9 us
    all_to_all x1, waiting for transfers between devices, one_device(): lax.all_to_all(sent, 'tile', split_axis=0, concat_axis=0, tiled=True)  11.3 us
    pallas_call x8, Pallas kernels, run(): return built(len(operands))(*operands)  9.61 us
    ppermute x1, starting transfers between devices, one_device(): lax.ppermute(jnp.where(upper, eastward, westward), 'tile', [(i, (i + (2 *...  7.1 us
    ppermute x1, starting transfers between devices, one_device(): from_south = lax.ppermute(northward, 'tile', steps_up)  4.99 us
  transfers between devices with their start and end apart: 15, of which 11 were waited for; matrix products, arithmetic and copies ran while one was open for 1% of the time, Pallas kernels for 4%

profile of v3, /device:TPU:1, one launch (start us, length us, event | category | flops | bytes accessed | tf_op | source)
XLA Modules:
  0.0 141.2 jit_solution(10404595497270883020)
XLA Ops:
  1.5 1.3 collective-permute-start.1
  3.1 5.0 %collective-permute-start = (bf16[118,128]{1,0:T(8,128)(2,1)S(1)}, bf16[118,128]{1,0:T(8,128)(2,1)S(1)}, u32[]{:S(2)}, u32[]{:S(2)}) collective-permute-start(bf16[118,128]{1,0:T(8,128)(2,1)S(1)} %pad_maximum_fusion.2), channel_id=1, source_target_pairs={{0,1},{1,2},{2,3},{3,4},{4,5},{5,6},{6,7},{8,9},{9,10},{10,11},{11... | collective-permute-start | bytes 90632 | tf_op jit(solution)/shard_map/ppermute | solution.py:449
  9.8 7.1 %collective-permute-start.2 = (bf16[130,128]{1,0:T(8,128)(2,1)S(1)}, bf16[130,128]{1,0:T(8,128)(2,1)S(1)}, u32[]{:S(2)}, u32[]{:S(2)}) collective-permute-start(bf16[130,128]{1,0:T(8,128)(2,1)S(1)} %maximum_select_fusion.1), channel_id=1, source_target_pairs={{0,112},{1,113},{2,114},{3,115},{4,116},{5,117},{6,118},{7,119},{8... | collective-permute-start | bytes 99848 | tf_op jit(solution)/shard_map/ppermute | solution.py:465
  17.9 15.5 %collective-permute-start.3 = (bf16[2,130,128]{2,1,0:T(8,128)(2,1)S(1)}, bf16[2,130,128]{2,1,0:T(8,128)(2,1)S(1)}, u32[]{:S(2)}, u32[]{:S(2)}) collective-permute-start(bf16[2,130,128]{2,1,0:T(8,128)(2,1)S(1)} %pad_maximum_fusion.1), channel_id=1, source_target_pairs={{0,8},{1,9},{2,10},{3,11},{4,12},{5,13},{6,14},{7,15},{8,0},{9,1},... | collective-permute-start | bytes 199688 | tf_op jit(solution)/shard_map/ppermute | solution.py:337
  34.6 11.9 %all-to-all-start = ((f32[128,1,128]{2,1,0:T(1,128)}), f32[128,1,128]{2,1,0:T(1,128)S(1)}, u32[]{:S(2)}, u32[]{:S(2)}) async-start(f32[128,1,128]{2,1,0:T(1,128)} %bitcast.30), calls=%async_computation | async-start | bytes 131072 | tf_op jit(solution)/shard_map/all_to_all | solution.py:439
  46.6 4.1 %shard_map.101 = (f32[30,40,128]{2,1,0:T(8,128)S(1)}, f32[8,48,128]{2,1,0:T(8,128)S(1)}, bf16[256,256]{1,0:T(8,128)(2,1)S(1)}, bf16[256,128]{1,0:T(8,128)(2,1)S(1)}) custom-call(bf16[36,36,128]{2,1,0:T(8,128)(2,1)S(1)} %get-tuple-element.23.forcing_ref, bf16[3,36,128]{2,1,0:T(8,128)(2,1)S(1)} %reshape.160.south_ref, ...), custom_call_target="tpu_custom_call" | custom-call | tf_op jit(solution)/shard_map/pallas_call | solution.py:314
  51.1 11.3 %all-to-all-done = f32[128,1,128]{2,1,0:T(1,128)S(1)} async-done(((f32[128,1,128]{2,1,0:T(1,128)}), f32[128,1,128]{2,1,0:T(1,128)S(1)}, u32[]{:S(2)}, u32[]{:S(2)}) %all-to-all-start) | async-done | bytes 65568 | tf_op jit(solution)/shard_map/all_to_all | solution.py:439
  63.9 2.3 %collective-permute-start.4 = (f32[2,40,128]{2,1,0:T(8,128)S(1)}, f32[2,40,128]{2,1,0:T(8,128)S(1)}, u32[]{:S(2)}, u32[]{:S(2)}) collective-permute-start(f32[2,40,128]{2,1,0:T(8,128)S(1)} %get-tuple-element.32), channel_id=1, source_target_pairs={{0,8},{1,9},{2,10},{3,11},{4,12},{5,13},{6,14},{7,15},{8,0},{9,1},... | collective-permute-start | bytes 122888 | tf_op jit(solution)/shard_map/ppermute | solution.py:337
  66.3 11.2 %collective-permute-done.4.r0 = f32[2,40,128]{2,1,0:T(8,128)S(1)} collective-permute-done((f32[2,40,128]{2,1,0:T(8,128)S(1)}, f32[2,40,128]{2,1,0:T(8,128)S(1)}, u32[]{:S(2)}, u32[]{:S(2)}) %collective-permute-start.4) | collective-permute-done | bytes 40992 | tf_op jit(solution)/shard_map/ppermute | solution.py:337
  77.5 2.3 %collective-permute-start.5 = (f32[2,40,128]{2,1,0:T(8,128)S(1)}, f32[2,40,128]{2,1,0:T(8,128)S(1)}, u32[]{:S(2)}, u32[]{:S(2)}) collective-permute-start(f32[2,40,128]{2,1,0:T(8,128)S(1)} %multiply_add_fusion.4), channel_id=1, source_target_pairs={{0,16},{1,17},{2,18},{3,19},{4,20},{5,21},{6,22},{7,23},{8,24},{9,... | collective-permute-start | bytes 122888 | tf_op jit(solution)/shard_map/ppermute | solution.py:337
  79.9 3.9 %collective-permute-done.5.r1 = f32[2,40,128]{2,1,0:T(8,128)S(1)} collective-permute-done((f32[2,40,128]{2,1,0:T(8,128)S(1)}, f32[2,40,128]{2,1,0:T(8,128)S(1)}, u32[]{:S(2)}, u32[]{:S(2)}) %collective-permute-start.5) | collective-permute-done | bytes 40992 | tf_op jit(solution)/shard_map/ppermute | solution.py:337
  83.8 2.4 %collective-permute-start.6 = (f32[2,40,128]{2,1,0:T(8,128)S(1)}, f32[2,40,128]{2,1,0:T(8,128)S(1)}, u32[]{:S(2)}, u32[]{:S(2)}) collective-permute-start(f32[2,40,128]{2,1,0:T(8,128)S(1)} %multiply_add_fusion.3), channel_id=1, source_target_pairs={{0,32},{1,33},{2,34},{3,35},{4,36},{5,37},{6,38},{7,39},{8,40},{9,... | collective-permute-start | bytes 122888 | tf_op jit(solution)/shard_map/ppermute | solution.py:337
  87.0 1.5 %collective-permute-done.6.r2 = f32[2,40,128]{2,1,0:T(8,128)S(1)} collective-permute-done((f32[2,40,128]{2,1,0:T(8,128)S(1)}, f32[2,40,128]{2,1,0:T(8,128)S(1)}, u32[]{:S(2)}, u32[]{:S(2)}) %collective-permute-start.6) | collective-permute-done | bytes 40992 | tf_op jit(solution)/shard_map/ppermute | solution.py:337
  88.5 2.3 %collective-permute-start.7 = (f32[2,40,128]{2,1,0:T(8,128)S(1)}, f32[2,40,128]{2,1,0:T(8,128)S(1)}, u32[]{:S(2)}, u32[]{:S(2)}) collective-permute-start(f32[2,40,128]{2,1,0:T(8,128)S(1)} %multiply_add_fusion.2), channel_id=1, source_target_pairs={{0,64},{1,65},{2,66},{3,67},{4,68},{5,69},{6,70},{7,71},{8,72},{9,... | collective-permute-start | bytes 122888 | tf_op jit(solution)/shard_map/ppermute | solution.py:337
  90.9 3.9 %collective-permute-done.7.r3 = f32[2,40,128]{2,1,0:T(8,128)S(1)} collective-permute-done((f32[2,40,128]{2,1,0:T(8,128)S(1)}, f32[2,40,128]{2,1,0:T(8,128)S(1)}, u32[]{:S(2)}, u32[]{:S(2)}) %collective-permute-start.7) | collective-permute-done | bytes 40992 | tf_op jit(solution)/shard_map/ppermute | solution.py:337
  95.3 3.1 %collective-permute-start.8 = (f32[2,40,128]{2,1,0:T(8,128)S(1)}, f32[2,40,128]{2,1,0:T(8,128)S(1)}, u32[]{:S(2)}, u32[]{:S(2)}) collective-permute-start(f32[2,40,128]{2,1,0:T(8,128)S(1)} %get-tuple-element.39), channel_id=1, source_target_pairs={{0,1},{1,0},{2,3},{3,2},{4,5},{5,4},{6,7},{7,6},{8,9},{9,8},{10,11... | collective-permute-start | bytes 122888 | tf_op jit(solution)/shard_map/ppermute | solution.py:337
  98.4 1.6 %collective-permute-done.8.r0 = f32[2,40,128]{2,1,0:T(8,128)S(1)} collective-permute-done((f32[2,40,128]{2,1,0:T(8,128)S(1)}, f32[2,40,128]{2,1,0:T(8,128)S(1)}, u32[]{:S(2)}, u32[]{:S(2)}) %collective-permute-start.8) | collective-permute-done | bytes 40992 | tf_op jit(solution)/shard_map/ppermute | solution.py:337
  100.0 2.3 %collective-permute-start.9 = (f32[2,40,128]{2,1,0:T(8,128)S(1)}, f32[2,40,128]{2,1,0:T(8,128)S(1)}, u32[]{:S(2)}, u32[]{:S(2)}) collective-permute-start(f32[2,40,128]{2,1,0:T(8,128)S(1)} %multiply_add_fusion.1), channel_id=1, source_target_pairs={{0,2},{1,3},{2,0},{3,1},{4,6},{5,7},{6,4},{7,5},{8,10},{9,11},{10,... | collective-permute-start | bytes 122888 | tf_op jit(solution)/shard_map/ppermute | solution.py:337
  102.4 3.3 %collective-permute-done.9.r1 = f32[2,40,128]{2,1,0:T(8,128)S(1)} collective-permute-done((f32[2,40,128]{2,1,0:T(8,128)S(1)}, f32[2,40,128]{2,1,0:T(8,128)S(1)}, u32[]{:S(2)}, u32[]{:S(2)}) %collective-permute-start.9) | collective-permute-done | bytes 40992 | tf_op jit(solution)/shard_map/ppermute | solution.py:337
  105.7 2.4 %collective-permute-start.10 = (f32[2,40,128]{2,1,0:T(8,128)S(1)}, f32[2,40,128]{2,1,0:T(8,128)S(1)}, u32[]{:S(2)}, u32[]{:S(2)}) collective-permute-start(f32[2,40,128]{2,1,0:T(8,128)S(1)} %multiply_add_fusion), channel_id=1, source_target_pairs={{0,4},{1,5},{2,6},{3,7},{4,0},{5,1},{6,2},{7,3},{8,12},{9,13},{10,... | collective-permute-start | bytes 122888 | tf_op jit(solution)/shard_map/ppermute | solution.py:337
  108.1 6.7 %collective-permute-done.10.r2 = f32[2,40,128]{2,1,0:T(8,128)S(1)} collective-permute-done((f32[2,40,128]{2,1,0:T(8,128)S(1)}, f32[2,40,128]{2,1,0:T(8,128)S(1)}, u32[]{:S(2)}, u32[]{:S(2)}) %collective-permute-start.10) | collective-permute-done | bytes 40992 | tf_op jit(solution)/shard_map/ppermute | solution.py:337
  115.0 2.2 %collective-permute-start.12 = (bf16[1296,128]{1,0:T(8,128)(2,1)S(1)}, bf16[1296,128]{1,0:T(8,128)(2,1)S(1)}, u32[]{:S(2)}, u32[]{:S(2)}) collective-permute-start(bf16[1296,128]{1,0:T(8,128)(2,1)S(1)} %shard_map.106.p0), channel_id=1, source_target_pairs={{0,256},{128,384},{256,0},{384,128},{1,257},{129,385},{257,1},{385... | collective-permute-start | bytes 995336 | tf_op jit(solution)/shard_map/ppermute | solution.py:337
  117.1 15.2 %collective-permute-start.11 = (bf16[1296,128]{1,0:T(8,128)(2,1)S(1)}, bf16[1296,128]{1,0:T(8,128)(2,1)S(1)}, u32[]{:S(2)}, u32[]{:S(2)}) collective-permute-start(bf16[1296,128]{1,0:T(8,128)(2,1)S(1)} %shard_map.106.p0), channel_id=1, source_target_pairs={{0,128},{128,0},{256,384},{384,256},{1,129},{129,1},{257,385},{385... | collective-permute-start | bytes 995336 | tf_op jit(solution)/shard_map/ppermute | solution.py:337
  132.4 6.5 %collective-permute-start.13 = (bf16[1296,128]{1,0:T(8,128)(2,1)S(1)}, bf16[1296,128]{1,0:T(8,128)(2,1)S(1)}, u32[]{:S(2)}, u32[]{:S(2)}) collective-permute-start(bf16[1296,128]{1,0:T(8,128)(2,1)S(1)} %collective-permute-done.12.p2), channel_id=1, source_target_pairs={{0,128},{128,0},{256,384},{384,256},{1,129},{129,1},{257,385},{385... | collective-permute-start | bytes 995336 | tf_op jit(solution)/shard_map/ppermute | solution.py:337
  (84 shorter events, 11.3 us)
Async XLA Ops:
  1.5 6.6 %collective-permute-start.1 = (bf16[118,128]{1,0:T(8,128)(2,1)S(1)}, bf16[118,128]{1,0:T(8,128)(2,1)S(1)}, u32[]{:S(2)}, u32[]{:S(2)}) collective-permute-start(bf16[118,128]{1,0:T(8,128)(2,1)S(1)} %pad_maximum_fusion.3), channel_id=1, source_target_pairs={{1,0},{2,1},{3,2},{4,3},{5,4},{6,5},{7,6},{9,8},{10,9},{11,10},{12... | collective-permute-start | bytes 90632 | tf_op jit(solution)/shard_map/ppermute | solution.py:450
  3.1 6.0 %collective-permute-start = (bf16[118,128]{1,0:T(8,128)(2,1)S(1)}, bf16[118,128]{1,0:T(8,128)(2,1)S(1)}, u32[]{:S(2)}, u32[]{:S(2)}) collective-permute-start(bf16[118,128]{1,0:T(8,128)(2,1)S(1)} %pad_maximum_fusion.2), channel_id=1, source_target_pairs={{0,1},{1,2},{2,3},{3,4},{4,5},{5,6},{6,7},{8,9},{9,10},{10,11},{11... | collective-permute-start | bytes 90632 | tf_op jit(solution)/shard_map/ppermute | solution.py:449
  9.8 8.1 %collective-permute-start.2 = (bf16[130,128]{1,0:T(8,128)(2,1)S(1)}, bf16[130,128]{1,0:T(8,128)(2,1)S(1)}, u32[]{:S(2)}, u32[]{:S(2)}) collective-permute-start(bf16[130,128]{1,0:T(8,128)(2,1)S(1)} %maximum_select_fusion.1), channel_id=1, source_target_pairs={{0,112},{1,113},{2,114},{3,115},{4,116},{5,117},{6,118},{7,119},{8... | collective-permute-start | bytes 99848 | tf_op jit(solution)/shard_map/ppermute | solution.py:465
  17.9 32.7 %collective-permute-start.3 = (bf16[2,130,128]{2,1,0:T(8,128)(2,1)S(1)}, bf16[2,130,128]{2,1,0:T(8,128)(2,1)S(1)}, u32[]{:S(2)}, u32[]{:S(2)}) collective-permute-start(bf16[2,130,128]{2,1,0:T(8,128)(2,1)S(1)} %pad_maximum_fusion.1), channel_id=1, source_target_pairs={{0,8},{1,9},{2,10},{3,11},{4,12},{5,13},{6,14},{7,15},{8,0},{9,1},... | collective-permute-start | bytes 199688 | tf_op jit(solution)/shard_map/ppermute | solution.py:337
  34.6 27.8 %all-to-all-start = ((f32[128,1,128]{2,1,0:T(1,128)}), f32[128,1,128]{2,1,0:T(1,128)S(1)}, u32[]{:S(2)}, u32[]{:S(2)}) async-start(f32[128,1,128]{2,1,0:T(1,128)} %bitcast.30), calls=%async_computation | async-start | bytes 131072 | tf_op jit(solution)/shard_map/all_to_all | solution.py:439
  63.9 13.5 %collective-permute-start.4 = (f32[2,40,128]{2,1,0:T(8,128)S(1)}, f32[2,40,128]{2,1,0:T(8,128)S(1)}, u32[]{:S(2)}, u32[]{:S(2)}) collective-permute-start(f32[2,40,128]{2,1,0:T(8,128)S(1)} %get-tuple-element.32), channel_id=1, source_target_pairs={{0,8},{1,9},{2,10},{3,11},{4,12},{5,13},{6,14},{7,15},{8,0},{9,1},... | collective-permute-start | bytes 122888 | tf_op jit(solution)/shard_map/ppermute | solution.py:337
  77.5 6.3 %collective-permute-start.5 = (f32[2,40,128]{2,1,0:T(8,128)S(1)}, f32[2,40,128]{2,1,0:T(8,128)S(1)}, u32[]{:S(2)}, u32[]{:S(2)}) collective-permute-start(f32[2,40,128]{2,1,0:T(8,128)S(1)} %multiply_add_fusion.4), channel_id=1, source_target_pairs={{0,16},{1,17},{2,18},{3,19},{4,20},{5,21},{6,22},{7,23},{8,24},{9,... | collective-permute-start | bytes 122888 | tf_op jit(solution)/shard_map/ppermute | solution.py:337
  83.7 2.4 %copy-start.1 = (f32[128]{0:T(128)S(1)}, f32[128]{0:T(128)}, u32[]{:S(2)}) copy-start(f32[128]{0:T(128)} %param.18) | copy-start | bytes 1540
  83.8 4.7 %collective-permute-start.6 = (f32[2,40,128]{2,1,0:T(8,128)S(1)}, f32[2,40,128]{2,1,0:T(8,128)S(1)}, u32[]{:S(2)}, u32[]{:S(2)}) collective-permute-start(f32[2,40,128]{2,1,0:T(8,128)S(1)} %multiply_add_fusion.3), channel_id=1, source_target_pairs={{0,32},{1,33},{2,34},{3,35},{4,36},{5,37},{6,38},{7,39},{8,40},{9,... | collective-permute-start | bytes 122888 | tf_op jit(solution)/shard_map/ppermute | solution.py:337
  88.5 6.3 %collective-permute-start.7 = (f32[2,40,128]{2,1,0:T(8,128)S(1)}, f32[2,40,128]{2,1,0:T(8,128)S(1)}, u32[]{:S(2)}, u32[]{:S(2)}) collective-permute-start(f32[2,40,128]{2,1,0:T(8,128)S(1)} %multiply_add_fusion.2), channel_id=1, source_target_pairs={{0,64},{1,65},{2,66},{3,67},{4,68},{5,69},{6,70},{7,71},{8,72},{9,... | collective-permute-start | bytes 122888 | tf_op jit(solution)/shard_map/ppermute | solution.py:337
  95.3 4.7 %collective-permute-start.8 = (f32[2,40,128]{2,1,0:T(8,128)S(1)}, f32[2,40,128]{2,1,0:T(8,128)S(1)}, u32[]{:S(2)}, u32[]{:S(2)}) collective-permute-start(f32[2,40,128]{2,1,0:T(8,128)S(1)} %get-tuple-element.39), channel_id=1, source_target_pairs={{0,1},{1,0},{2,3},{3,2},{4,5},{5,4},{6,7},{7,6},{8,9},{9,8},{10,11... | collective-permute-start | bytes 122888 | tf_op jit(solution)/shard_map/ppermute | solution.py:337
  100.0 5.6 %collective-permute-start.9 = (f32[2,40,128]{2,1,0:T(8,128)S(1)}, f32[2,40,128]{2,1,0:T(8,128)S(1)}, u32[]{:S(2)}, u32[]{:S(2)}) collective-permute-start(f32[2,40,128]{2,1,0:T(8,128)S(1)} %multiply_add_fusion.1), channel_id=1, source_target_pairs={{0,2},{1,3},{2,0},{3,1},{4,6},{5,7},{6,4},{7,5},{8,10},{9,11},{10,... | collective-permute-start | bytes 122888 | tf_op jit(solution)/shard_map/ppermute | solution.py:337
  105.7 9.1 %collective-permute-start.10 = (f32[2,40,128]{2,1,0:T(8,128)S(1)}, f32[2,40,128]{2,1,0:T(8,128)S(1)}, u32[]{:S(2)}, u32[]{:S(2)}) collective-permute-start(f32[2,40,128]{2,1,0:T(8,128)S(1)} %multiply_add_fusion), channel_id=1, source_target_pairs={{0,4},{1,5},{2,6},{3,7},{4,0},{5,1},{6,2},{7,3},{8,12},{9,13},{10,... | collective-permute-start | bytes 122888 | tf_op jit(solution)/shard_map/ppermute | solution.py:337
  114.8 25.3 %copy-start = (bf16[1,1,36,36,128]{4,3,2,1,0:T(8,128)(2,1)S(1)}, bf16[1,1,36,36,128]{4,3,2,1,0:T(8,128)(2,1)}, u32[]{:S(2)}) copy-start(bf16[1,1,36,36,128]{4,3,2,1,0:T(8,128)(2,1)} %param.19) | copy-start | bytes 995332
  115.0 17.4 %collective-permute-start.12 = (bf16[1296,128]{1,0:T(8,128)(2,1)S(1)}, bf16[1296,128]{1,0:T(8,128)(2,1)S(1)}, u32[]{:S(2)}, u32[]{:S(2)}) collective-permute-start(bf16[1296,128]{1,0:T(8,128)(2,1)S(1)} %shard_map.106.p0), channel_id=1, source_target_pairs={{0,256},{128,384},{256,0},{384,128},{1,257},{129,385},{257,1},{385... | collective-permute-start | bytes 995336 | tf_op jit(solution)/shard_map/ppermute | solution.py:337
  117.1 21.7 %collective-permute-start.11 = (bf16[1296,128]{1,0:T(8,128)(2,1)S(1)}, bf16[1296,128]{1,0:T(8,128)(2,1)S(1)}, u32[]{:S(2)}, u32[]{:S(2)}) collective-permute-start(bf16[1296,128]{1,0:T(8,128)(2,1)S(1)} %shard_map.106.p0), channel_id=1, source_target_pairs={{0,128},{128,0},{256,384},{384,256},{1,129},{129,1},{257,385},{385... | collective-permute-start | bytes 995336 | tf_op jit(solution)/shard_map/ppermute | solution.py:337
  132.4 7.8 %collective-permute-start.13 = (bf16[1296,128]{1,0:T(8,128)(2,1)S(1)}, bf16[1296,128]{1,0:T(8,128)(2,1)S(1)}, u32[]{:S(2)}, u32[]{:S(2)}) collective-permute-start(bf16[1296,128]{1,0:T(8,128)(2,1)S(1)} %collective-permute-done.12.p2), channel_id=1, source_target_pairs={{0,128},{128,0},{256,384},{384,256},{1,129},{129,1},{257,385},{385... | collective-permute-start | bytes 995336 | tf_op jit(solution)/shard_map/ppermute | solution.py:337
